TPU v7x, 256 devices: a whole 4x4x8 slice. The times are simulated.
256 devices in a mesh: replica: 4 (over z_lo), fsdp: 64 (over y, z_hi, x, core).
Axes of the slice: x: 4, y: 4, z: 8 (z_hi: 2, z_lo: 4; z = z_hi * 4 + z_lo), core: 2. Of those that a mesh axis runs over, the one named last changes fastest.
Arguments:
- tokens: bfloat16 [131072, 8192], P(('replica', 'fsdp')), may hold values from -24 to 24
- cotangent: bfloat16 [131072, 512], P(('replica', 'fsdp')), may hold values from -4 to 4
- z_weights: float32 [8192, 512], P('fsdp'), may hold values from -6 to 6
- x_weights: float32 [8192, 512], P('fsdp'), may hold values from -6 to 6
- second_moment: float32 [8192, 512], P('fsdp'), may hold values from 0.3 to 3
Outputs:
- values: bfloat16 [131072, 512], P(('replica', 'fsdp'))
- z_next: float32 [8192, 512], P('fsdp')
- x_next: float32 [8192, 512], P('fsdp')
- second_next: float32 [8192, 512], P('fsdp')
All inputs are finite; a program needn't handle non-finite values.
Results may differ from a plain program's by a relative error of at most 0.0049.
Values may be sent and summed in bfloat16 or wider, within the bound.
A program may use at most 128 MiB of HBM per device.

v0:
```python
import math

import jax
import jax.numpy as jnp
from jax import lax
from jax.sharding import PartitionSpec as P

beta_first = 0.9
beta_second = 0.95
learn_rate = 0.25
weight_decay = 0.1
step_count = 8.0
epsilon = 1e-08
bias_fix = 1.0 - 0.95**8
mixing = 1.0 / (step_count + 1.0)


def update(gradient, z_weights, x_weights, second_moment, blended):
    second_next = beta_second * second_moment + (1.0 - beta_second) * gradient * gradient
    scaled = gradient / (jnp.sqrt(second_next / bias_fix) + epsilon)
    z_next = z_weights - learn_rate * (scaled + weight_decay * blended)
    x_next = (1.0 - mixing) * x_weights + mixing * z_next
    return (z_next, x_next, second_next)


def local(tokens, cotangent, z_weights, x_weights, second_moment):
    model_width = tokens.shape[1]
    norm_factor = 1.0 / math.sqrt(model_width)
    blended = (1.0 - beta_first) * z_weights + beta_first * x_weights
    weights = blended.astype(jnp.bfloat16)
    columns = tokens
    summed = jnp.dot(
        columns,
        lax.all_gather(weights, "fsdp", axis=0, tiled=True),
        preferred_element_type=jnp.float32,
    )
    values = (summed * norm_factor).astype(jnp.bfloat16)
    columns = tokens
    partial_sum = lax.psum_scatter(
        jnp.einsum("td,th->dh", columns, cotangent, preferred_element_type=jnp.float32)
        * norm_factor,
        "fsdp",
        scatter_dimension=0,
        tiled=True,
    )
    gradient = lax.psum(partial_sum.astype(jnp.bfloat16), "replica").astype(jnp.float32)
    z_next, x_next, second_next = update(gradient, z_weights, x_weights, second_moment, blended)
    return (values, z_next, x_next, second_next)


def solution(mesh):
    return jax.shard_map(
        local,
        mesh=mesh,
        in_specs=(
            P(("replica", "fsdp"), None),
            P(("replica", "fsdp"), None),
            P("fsdp", None),
            P("fsdp", None),
            P("fsdp", None),
        ),
        out_specs=(P(("replica", "fsdp"), None), P("fsdp", None), P("fsdp", None), P("fsdp", None)),
        check_vma=False,
    )
```

profile of v0, /device:TPU:32, one launch (start us, length us, event | category | flops | bytes accessed | tf_op | source)
XLA Modules:
  0.0 651.2 jit_solution(10585263623006494585)
XLA Ops:
  7.2 0.0 copy-start
  7.2 0.0 reduce-scatter.2.cloned.1.call-start
  7.2 1.0 copy-done
  8.2 11.7 %convolution_multiply_fusion = f32[8192,512]{1,0:T(8,128)} fusion(bf16[512,8192]{1,0:T(8,128)(2,1)} %param.5, bf16[512,512]{1,0:T(8,128)(2,1)S(1)} %copy-done), kind=kOutput, calls=%fused_computation | convolution fusion | flops 4299161600 | bytes 25690112 | tf_op jit(solution)/shard_map/td,th->dh/dot_general | solution.py:40
  19.9 0.0 copy-start.1
  19.9 0.0 copy-start.2
  19.9 0.0 copy-start.3
  19.9 0.0 reduce-scatter.2.cloned.1.call-update
  19.9 0.0 all-reduce.2.cloned.1.call-start
  19.9 446.1 %reduce-scatter.2.cloned.1.call-done = f32[128,512]{1,0:T(8,128)} async-done(((f32[8192,512]{1,0:T(8,128)}), f32[128,512]{1,0:T(8,128)}) %reduce-scatter.2.cloned.1.call-update) | async-done | bytes 262160 | tf_op jit(solution)/shard_map/reduce_scatter | solution.py:39
  466.1 1.6 convert_element_type.18
  467.7 0.0 all-reduce.2.cloned.1.call-update
  467.7 0.0 all-gather.2.cloned.1.call-start
  467.8 47.8 %all-reduce.2.cloned.1.call-done = bf16[128,512]{1,0:T(8,128)(2,1)} async-done(((bf16[128,512]{1,0:T(8,128)(2,1)}), bf16[128,512]{1,0:T(8,128)(2,1)}) %all-reduce.2.cloned.1.call-update) | async-done | bytes 131088 | tf_op jit(solution)/shard_map/psum | solution.py:46
  515.6 0.0 copy-done.1
  515.6 0.0 copy-done.2
  515.6 0.0 copy-done.3
  515.6 2.1 multiply_add_fusion
  517.6 0.0 all-gather.2.cloned.1.call-update
  517.7 115.7 %all-gather.2.cloned.1.call-done = bf16[8192,512]{1,0:T(8,128)(2,1)} async-done(((bf16[128,512]{1,0:T(8,128)(2,1)}), bf16[8192,512]{1,0:T(8,128)(2,1)}) %all-gather.2.cloned.1.call-update) | async-done | bytes 8388624 | tf_op jit(solution)/shard_map/all_gather | solution.py:34
  633.3 10.3 %fusion.1 = bf16[512,512]{0,1:T(8,128)(2,1)S(1)} fusion(bf16[8192,512]{1,0:T(8,128)(2,1)} %all-gather.2.cloned.1.call-done, bf16[512,8192]{1,0:T(8,128)(2,1)} %param.5), kind=kOutput, calls=%fused_computation.3 | convolution fusion | flops 4295491584 | bytes 17301504 | tf_op jit(solution)/shard_map/dot_general | solution.py:32
  643.6 1.0 copy.9
Async XLA Ops:
  7.2 1.0 copy-start
  7.2 458.9 %reduce-scatter.2.cloned.1.call-start = ((), (), s32[]{:S(2)}) async-start(), calls=%async_computation.2 | async-start | bytes 17039360 | tf_op jit(solution)/shard_map/reduce_scatter | solution.py:39
  19.9 495.7 %copy-start.1 = (f32[128,512]{1,0:T(8,128)S(1)}, f32[128,512]{1,0:T(8,128)}, u32[]{:S(2)}) copy-start(f32[128,512]{1,0:T(8,128)} %param.8) | copy-start | bytes 786436
  19.9 495.7 %copy-start.2 = (f32[128,512]{1,0:T(8,128)S(1)}, f32[128,512]{1,0:T(8,128)}, u32[]{:S(2)}) copy-start(f32[128,512]{1,0:T(8,128)} %param.7) | copy-start | bytes 786436
  19.9 495.7 %copy-start.3 = (f32[128,512]{1,0:T(8,128)S(1)}, f32[128,512]{1,0:T(8,128)}, u32[]{:S(2)}) copy-start(f32[128,512]{1,0:T(8,128)} %param.9) | copy-start | bytes 786436
  19.9 495.7 %all-reduce.2.cloned.1.call-start = ((), (), s32[]{:S(2)}) async-start(), calls=%async_computation.3 | async-start | bytes 262144 | tf_op jit(solution)/shard_map/psum | solution.py:46
  467.7 165.6 %all-gather.2.cloned.1.call-start = ((), (), s32[]{:S(2)}) async-start(), calls=%async_computation.1 | async-start | bytes 8519680 | tf_op jit(solution)/shard_map/all_gather | solution.py:34
Sparse Core Ops, SparseCore 0:
  20.0 446.0 reduce-scatter.1
  469.3 46.2 all-reduce.1
  520.4 112.8 all-gather.1
where the time goes:
time: 654 us; the launch traced here: 651 us
  waiting for transfers between devices  610 us (93%)
  matrix products  22 us (3%)
  between operations  13.8 us (2%)
    reduce_scatter x1, waiting for transfers between devices, local(): lax.psum_scatter(jnp.einsum('td,th->dh', columns, cotangent, preferred_el...  446 us
    all_gather x1, waiting for transfers between devices, local(): lax.all_gather(weights, 'fsdp', axis=0, tiled=True)  116 us
    psum x1, waiting for transfers between devices, local(): lax.psum(partial_sum.astype(jnp.bfloat16), 'replica').astype(jnp.float32)  47.8 us
  transfers between devices with their start and end apart: 3, of which 3 were waited for; matrix products, arithmetic and copies ran while one was open for 0% of the time, Pallas kernels for 0%

commit v1 on v0

v1 whole, which is shorter than its diff:
```python
import math

import jax
import jax.numpy as jnp
from jax import lax
from jax.experimental import pallas as pl
from jax.experimental.pallas import tpu as pltpu
from jax.sharding import PartitionSpec as P

beta_first = 0.9
beta_second = 0.95
learn_rate = 0.25
weight_decay = 0.1
step_count = 8.0
epsilon = 1e-08
bias_fix = 1.0 - 0.95**8
mixing = 1.0 / (step_count + 1.0)

D = 8192
HV = 512
TOK = 512
NORM = 1.0 / math.sqrt(D)
F32 = jnp.float32
BF16 = jnp.bfloat16
MESH = pl.DeviceIdType.MESH
N_MSG = 84


def kernel(
    tokens, cot_hbm, z_ref, x_ref, s_ref,
    values_out, z_out, x_out, s_out,
    tok, cot, cot_t, wts, gt,
    relay1, direct1, summed1, stage1, g1f, g1b,
    relay2, direct2, summed2, stage2, plane, zstage, zrecv, gfull, acc, vrecv,
    send_sem, recv_sem, tok_local, tok_send, tok_recv, cot_sem,
):
    zl = lax.axis_index("replica")
    index = lax.axis_index("fsdp")
    core = lax.rem(index, 2)
    xc = lax.rem(index // 2, 4)
    zh = lax.rem(index // 8, 2)
    yc = index // 16

    def fsdp_of(y, h, x):
        return ((y * 2 + h) * 4 + x) * 2 + core

    def mod4(v):
        return lax.rem(v + 8, 4)

    partner = (zl, index + 1 - 2 * core)
    x_side = [(zl, fsdp_of(yc, zh, mod4(xc + d))) for d in (1, -1)]
    y_side = [(zl, fsdp_of(mod4(yc + d), zh, xc)) for d in (1, -1)]
    z_now = zh * 4 + zl

    def z_dev(z):
        return (lax.rem(z, 4), fsdp_of(yc, z // 4, xc))

    z_peers = [z_dev(lax.rem(z_now + k, 8)) for k in range(1, 8)]
    mirror = z_dev(7 - z_now)

    barrier = pltpu.get_barrier_semaphore()
    for dev in [partner] + x_side + y_side + z_peers:
        pl.semaphore_signal(barrier, inc=1, device_id=dev, device_id_type=MESH)

    def local_tok(b):
        col = pl.multiple_of((2 * b + core) * 128, 128)
        dst_col = pl.multiple_of(lax.rem(b, 8) * 128, 128)
        return pltpu.make_async_copy(
            tokens.at[:, pl.ds(col, 128)],
            tok.at[b // 8, 0, :, pl.ds(dst_col, 128)],
            tok_local.at[b],
        )

    def remote_tok(b):
        col = pl.multiple_of((2 * b + 1 - core) * 128, 128)
        dst_col = pl.multiple_of(lax.rem(b, 8) * 128, 128)
        return pltpu.make_async_remote_copy(
            src_ref=tokens.at[:, pl.ds(col, 128)],
            dst_ref=tok.at[b // 8, 1, :, pl.ds(dst_col, 128)],
            send_sem=tok_send.at[b],
            recv_sem=tok_recv.at[b],
            device_id=partner,
            device_id_type=MESH,
        )

    cot_local = pltpu.make_async_copy(cot_hbm, cot.at[0], cot_sem)
    cot_local.start()

    @pl.loop(0, 32)
    def _(b):
        local_tok(b).start()

    blended = (1.0 - beta_first) * z_ref[...] + beta_first * x_ref[...]
    wts[yc, zh, xc] = blended.astype(BF16)

    pl.semaphore_wait(barrier, 12)

    sends = []
    counter = [0]

    def message(src, dst, dev):
        m = counter[0]
        counter[0] += 1
        copy = pltpu.make_async_remote_copy(
            src_ref=src, dst_ref=dst, send_sem=send_sem.at[m], recv_sem=recv_sem.at[m],
            device_id=dev, device_id_type=MESH,
        )
        copy.start()
        sends.append(copy)
        return m

    def arrived(m, dst):
        pltpu.make_async_remote_copy(
            src_ref=dst, dst_ref=dst, send_sem=send_sem.at[m], recv_sem=recv_sem.at[m],
            device_id=partner, device_id_type=MESH,
        ).wait_recv()

    first = (xc, yc)
    second = (yc, xc)
    first_side = (x_side, y_side)
    second_side = (y_side, x_side)

    def block(p, f, s, h, r0, rows):
        y, x = (s, f) if p == 0 else (f, s)
        return wts.at[y, h, x, pl.ds(r0, rows), :]

    def line(p, s, h, r0, rows):
        if p == 0:
            return wts.at[s, h, :, pl.ds(r0, rows), :]
        return wts.at[:, h, s, pl.ds(r0, rows), :]

    half_of = (zh, 1 - zh)
    ag = {}

    def ag0(st):
        h = half_of[st]
        for p in (0, 1):
            f, s, r0 = first[p], second[p], 64 * p
            own = block(p, f, s, h, r0, 64)
            for d in (0, 1):
                ag[st, p, 0, d] = message(own, own, first_side[p][d])

    def ag1(st):
        h = half_of[st]
        for p in (0, 1):
            f, s, r0 = first[p], second[p], 64 * p
            for d in (0, 1):
                src_f = mod4(f - 1 + 2 * d)
                arrived(ag[st, p, 0, d], block(p, src_f, s, h, r0, 64))
                part = block(p, src_f, s, h, r0 + 32 * d, 32)
                ag[st, p, 1, d] = message(part, part, first_side[p][d])

    def ag2(st):
        h = half_of[st]
        for p in (0, 1):
            f, s, r0 = first[p], second[p], 64 * p
            for d in (0, 1):
                arrived(ag[st, p, 1, d], block(p, mod4(f + 2), s, h, r0 + 32 * d, 32))
            row = line(p, s, h, r0, 64)
            for d in (0, 1):
                ag[st, p, 2, d] = message(row, row, second_side[p][d])

    def ag3(st):
        h = half_of[st]
        for p in (0, 1):
            s, r0 = second[p], 64 * p
            for d in (0, 1):
                src_s = mod4(s - 1 + 2 * d)
                arrived(ag[st, p, 2, d], line(p, src_s, h, r0, 64))
                part = line(p, src_s, h, r0 + 32 * d, 32)
                ag[st, p, 3, d] = message(part, part, second_side[p][d])

    def ag4(st):
        h = half_of[st]
        for p in (0, 1):
            s, r0 = second[p], 64 * p
            for d in (0, 1):
                arrived(ag[st, p, 3, d], line(p, mod4(s + 2), h, r0 + 32 * d, 32))

    cot_msg = message(cot_hbm, cot.at[1], partner)
    ag0(0)
    own = wts.at[yc, zh, xc]
    mirror_msg = message(own, own, mirror)

    @pl.loop(0, 32)
    def _(b):
        remote_tok(b).start()

    cot_local.wait()
    arrived(cot_msg, cot.at[1])
    for k in (0, 1):
        cot_t[:, 512 * k:512 * (k + 1)] = cot[k].T

    def grad_step(j):
        for b in (2 * j, 2 * j + 1):
            local_tok(b).wait()
            remote_tok(b).wait_recv()
        y, h, pair = j // 4, lax.rem(j // 2, 2), lax.rem(j, 2)
        col = pl.multiple_of(lax.rem(j, 4) * 256, 256)
        rhs = tok[y, :, :, pl.ds(col, 256)].reshape(1024, 256)
        for q in (0, 1):
            out = jnp.dot(cot_t[256 * q:256 * (q + 1), :], rhs, preferred_element_type=F32).astype(BF16)
            gt[y, h, 2 * pair, 256 * q:256 * (q + 1), :] = out[:, :128]
            gt[y, h, 2 * pair + 1, 256 * q:256 * (q + 1), :] = out[:, 128:]

    def grad(j0, j1):
        @pl.loop(j0, j1)
        def _(j):
            grad_step(j)

    ag1(0)
    grad(0, 2)
    arrived(mirror_msg, wts.at[yc, 1 - zh, xc])
    ag0(1)
    ag2(0)
    grad(2, 5)
    ag1(1)
    grad(5, 8)
    ag2(1)
    grad(8, 12)
    ag3(0)
    grad(12, 16)

    def gset(p, f, h):
        hv = pl.ds(256 * p, 256)
        if p == 0:
            return gt.at[:, h, f, hv, :]
        return gt.at[f, h, :, hv, :]

    def gblk(p, f, h, i):
        hv = pl.ds(256 * p, 256)
        if p == 0:
            return gt[i, h, f, hv, :].astype(F32)
        return gt[f, h, i, hv, :].astype(F32)

    def nxt(c, d):
        return mod4(c + 1 - 2 * d)

    rs = {}
    for p in (0, 1):
        for d in (0, 1):
            rs[p, 0, d] = message(gset(p, mod4(first[p] + 2), d), relay1.at[p, d], first_side[p][d])
    for p in (0, 1):
        for d in (0, 1):
            rs[p, 1, d] = message(gset(p, nxt(first[p], d), 1 - d), direct1.at[p, d], first_side[p][d])

    ag3(1)
    ag4(0)

    acc_first = [True]

    def values_step(y, m):
        lhs = tok[y, m]
        rhs = wts[y].reshape(1024, 512)
        acc[m] += jnp.dot(lhs, rhs, preferred_element_type=F32)

    acc[...] = jnp.zeros_like(acc)

    def rs1_c():
        for p in (0, 1):
            for d in (0, 1):
                arrived(rs[p, 0, d], relay1.at[p, d])

                @pl.loop(0, 4)
                def _(i):
                    stage1[p, d, i] = (gblk(p, nxt(first[p], d), d, i) + relay1[p, d, i].astype(F32)).astype(BF16)

                rs[p, 2, d] = message(stage1.at[p, d], summed1.at[p, d], first_side[p][d])

    rs1_c()
    ag4(1)

    def values(y0, y1):
        @pl.loop(y0, y1)
        def _(y):
            @pl.loop(0, 2)
            def _(m):
                values_step(y, m)

    values(0, 2)

    for p in (0, 1):
        for d in (0, 1):
            arrived(rs[p, 1, d], direct1.at[p, d])
            arrived(rs[p, 2, d], summed1.at[p, d])
        for h in (0, 1):
            @pl.loop(0, 4)
            def _(i):
                total = (
                    gblk(p, first[p], h, i)
                    + direct1[p, 1 - h, i].astype(F32)
                    + summed1[p, h, i].astype(F32)
                )
                g1f[p, i, h] = total
                g1b[p, i, h] = total.astype(BF16)
        s = second[p]
        for d in (0, 1):
            rs[p, 3, d] = message(g1b.at[p, mod4(s + 2), d], relay2.at[p, d], second_side[p][d])
        for d in (0, 1):
            rs[p, 4, d] = message(g1b.at[p, nxt(s, d), 1 - d], direct2.at[p, d], second_side[p][d])

    values(2, 4)
    vmsg = message(acc.at[1], vrecv, partner)

    for p in (0, 1):
        for d in (0, 1):
            arrived(rs[p, 3, d], relay2.at[p, d])
            stage2[p, d] = (g1f[p, nxt(second[p], d), d] + relay2[p, d].astype(F32)).astype(BF16)
            rs[p, 5, d] = message(stage2.at[p, d], summed2.at[p, d], second_side[p][d])

    for p in (0, 1):
        for d in (0, 1):
            arrived(rs[p, 4, d], direct2.at[p, d])
            arrived(rs[p, 5, d], summed2.at[p, d])
        for h in (0, 1):
            total = g1f[p, second[p], h] + direct2[p, 1 - h].astype(F32) + summed2[p, h].astype(F32)
            plane[h, 256 * p:256 * (p + 1), :] = total
            zstage[h, 256 * p:256 * (p + 1), :] = total.astype(BF16)

    zmsgs = []
    for k in range(1, 8):
        dest = lax.rem(z_now + k, 8)
        piece = zstage.at[dest // 4, pl.ds(pl.multiple_of(lax.rem(dest, 4) * 128, 128), 128), :]
        zmsgs.append(message(piece, zrecv.at[k - 1], z_peers[k - 1]))

    arrived(vmsg, vrecv)
    values_out[...] = ((acc[0] + vrecv[...]) * NORM).astype(BF16)

    my_hv = pl.ds(pl.multiple_of(zl * 128, 128), 128)
    total = plane[zh, my_hv, :]
    for k in range(7):
        arrived(zmsgs[k], zrecv.at[k])
        total = total + zrecv[k].astype(F32)
    gfull[my_hv, :] = total
    rmsgs = []
    for k in range(1, 4):
        rmsgs.append(message(gfull.at[my_hv, :], gfull.at[my_hv, :], (lax.rem(zl + k, 4), index)))
    for k in range(1, 4):
        src = pl.multiple_of(lax.rem(zl + 4 - k, 4) * 128, 128)
        arrived(rmsgs[k - 1], gfull.at[pl.ds(src, 128), :])

    gradient = gfull[...].T * NORM
    z_in = z_ref[...]
    x_in = x_ref[...]
    mixed = (1.0 - beta_first) * z_in + beta_first * x_in
    second_next = beta_second * s_ref[...] + (1.0 - beta_second) * gradient * gradient
    scaled = gradient / (jnp.sqrt(second_next / bias_fix) + epsilon)
    z_next = z_in - learn_rate * (scaled + weight_decay * mixed)
    s_out[...] = second_next
    z_out[...] = z_next
    x_out[...] = (1.0 - mixing) * x_in + mixing * z_next

    for copy in sends:
        copy.wait_send()

    @pl.loop(0, 32)
    def _(b):
        remote_tok(b).wait_send()

    assert counter[0] <= N_MSG


def local(tokens, cotangent, z_weights, x_weights, second_moment):
    vm = pl.BlockSpec(memory_space=pltpu.VMEM)
    hbm = pl.BlockSpec(memory_space=pl.ANY)
    shard = jax.ShapeDtypeStruct((128, HV), F32)
    dma = pltpu.SemaphoreType.DMA
    return pl.pallas_call(
        kernel,
        out_shape=(jax.ShapeDtypeStruct((TOK, HV), BF16), shard, shard, shard),
        in_specs=[hbm, hbm, vm, vm, vm],
        out_specs=(vm, vm, vm, vm),
        scratch_shapes=[
            pltpu.VMEM((4, 2, 512, 1024), BF16),
            pltpu.VMEM((2, 512, 512), BF16),
            pltpu.VMEM((512, 1024), BF16),
            pltpu.VMEM((4, 2, 4, 128, 512), BF16),
            pltpu.VMEM((4, 2, 4, 512, 128), BF16),
            pltpu.VMEM((2, 2, 4, 256, 128), BF16),
            pltpu.VMEM((2, 2, 4, 256, 128), BF16),
            pltpu.VMEM((2, 2, 4, 256, 128), BF16),
            pltpu.VMEM((2, 2, 4, 256, 128), BF16),
            pltpu.VMEM((2, 4, 2, 256, 128), F32),
            pltpu.VMEM((2, 4, 2, 256, 128), BF16),
            pltpu.VMEM((2, 2, 256, 128), BF16),
            pltpu.VMEM((2, 2, 256, 128), BF16),
            pltpu.VMEM((2, 2, 256, 128), BF16),
            pltpu.VMEM((2, 2, 256, 128), BF16),
            pltpu.VMEM((2, 512, 128), F32),
            pltpu.VMEM((2, 512, 128), BF16),
            pltpu.VMEM((7, 128, 128), BF16),
            pltpu.VMEM((512, 128), F32),
            pltpu.VMEM((2, 512, 512), F32),
            pltpu.VMEM((512, 512), F32),
            dma((N_MSG,)),
            dma((N_MSG,)),
            dma((32,)),
            dma((32,)),
            dma((32,)),
            dma,
        ],
        compiler_params=pltpu.CompilerParams(
            collective_id=0, has_side_effects=True, vmem_limit_bytes=56 * 1024 * 1024
        ),
    )(tokens, cotangent, z_weights, x_weights, second_moment)


def solution(mesh):
    return jax.shard_map(
        local,
        mesh=mesh,
        in_specs=(
            P(("replica", "fsdp"), None),
            P(("replica", "fsdp"), None),
            P("fsdp", None),
            P("fsdp", None),
            P("fsdp", None),
        ),
        out_specs=(P(("replica", "fsdp"), None), P("fsdp", None), P("fsdp", None), P("fsdp", None)),
        check_vma=False,
    )
```

time: 654 us -> 87.7 us (0.13)
  waiting for transfers between devices: 610 us -> 0 us
  Pallas kernels: 0 us -> 80 us
  matrix products: 22 us -> 0 us
  between operations: 13.8 us -> 0.64 us
    reduce_scatter x1 -> x0, waiting for transfers between devices: 446 us -> none  [local(): lax.psum_scatter(jnp.einsum('td,th->dh', columns, cotangent, preferred_el...]
    all_gather x1 -> x0, waiting for transfers between devices: 116 us -> none  [local(): lax.all_gather(weights, 'fsdp', axis=0, tiled=True)]
    pallas_call x0 -> x1, Pallas kernels: none -> 80 us  [local(): pl.pallas_call(kernel, out_shape=(jax.ShapeDtypeStruct((TOK, HV), BF16),...]
    psum x1 -> x0, waiting for transfers between devices: 47.8 us -> none  [local(): lax.psum(partial_sum.astype(jnp.bfloat16), 'replica').astype(jnp.float32)]
    dot_general x2 -> x0, matrix products: 22 us -> none  [the longest x1 11.7 us: local(): jnp.einsum('td,th->dh', columns, cotangent, preferred_element_type=jnp.fl...]
  transfers between devices with their start and end apart: 3 -> 0, of which waited for: 3 -> 0; matrix products, arithmetic and copies ran while one was open for 0% -> 0% of each run, Pallas kernels for 0% -> 0%
where the time goes in v1:
time: 87.7 us; the launch traced here: 87.5 us
  Pallas kernels  80 us (91%)
  local copies, waits for them, and re-layouts  6.88 us (8%)
    pallas_call x1, Pallas kernels, local(): pl.pallas_call(kernel, out_shape=(jax.ShapeDtypeStruct((TOK, HV), BF16),...  80 us
    unnamed x4, local copies, waits for them, and re-layouts  6.88 us

profile of v1, /device:TPU:32, one launch (start us, length us, event | category | flops | bytes accessed | tf_op | source)
XLA Modules:
  0.0 87.5 jit_solution(3107514254155211522)
XLA Ops:
  0.6 80.0 %shard_map.84 = (bf16[512,512]{1,0:T(8,128)(2,1)}, f32[128,512]{1,0:T(8,128)}, f32[128,512]{1,0:T(8,128)}, f32[128,512]{1,0:T(8,128)}) custom-call(bf16[512,8192]{1,0:T(8,128)(2,1)} %tokens.1, bf16[512,512]{1,0:T(8,128)(2,1)} %cot_hbm.1, f32[128,512]{1,0:T(8,128)} %z_ref.1, f32[128,512]{1,0:T(8,128)} %x_ref.1, f32[128,512]{1,0:T(8,128)} %s_ref.1), custom_call_target="tpu_custom_call" | custom-call | tf_op jit(solution)/shard_map/pallas_call | solution.py:368
  80.6 1.9 %copy.13 = bf16[512,512]{1,0:T(8,128)(2,1)} copy(bf16[512,512]{1,0:T(8,128)(2,1)} %get-tuple-element.8) | data formatting | bytes 1048576
  82.5 1.7 %copy.14 = f32[128,512]{1,0:T(8,128)} copy(f32[128,512]{1,0:T(8,128)} %get-tuple-element.9) | data formatting | bytes 524288
  84.1 1.7 %copy.15 = f32[128,512]{1,0:T(8,128)} copy(f32[128,512]{1,0:T(8,128)} %get-tuple-element.10) | data formatting | bytes 524288
  85.8 1.7 %copy.16 = f32[128,512]{1,0:T(8,128)} copy(f32[128,512]{1,0:T(8,128)} %get-tuple-element.11) | data formatting | bytes 524288

commit v2 on v0

v2 whole, which is shorter than its diff:
```python
import math

import jax
import jax.numpy as jnp
from jax import lax
from jax.experimental import pallas as pl
from jax.experimental.pallas import tpu as pltpu
from jax.sharding import PartitionSpec as P

beta_first = 0.9
beta_second = 0.95
learn_rate = 0.25
weight_decay = 0.1
step_count = 8.0
epsilon = 1e-08
bias_fix = 1.0 - 0.95**8
mixing = 1.0 / (step_count + 1.0)

D = 8192
HV = 512
TOK = 512
NORM = 1.0 / math.sqrt(D)
F32 = jnp.float32
BF16 = jnp.bfloat16
MESH = pl.DeviceIdType.MESH
N_MSG = 176


def kernel(
    tokens, cot_hbm, z_hbm, x_hbm,
    values_out, grad_out,
    z_ref, x_ref, tok, cot, cot_t, wts, gt,
    relay1, direct1, summed1, stage1, g1f, g1b, relay2, direct2, summed2, stage2,
    c_f, c_b,
    c_relay1, c_direct1, c_summed1, c_stage1, c_g1f, c_g1b, c_relay2, c_direct2, c_summed2, c_stage2,
    zc_half, zc_recv, zc_stage,
    plane, zstage, zrecv, gfull, acc, vrecv,
    send_sem, recv_sem, tok_local, tok_send, tok_recv, in_sem,
):
    zl = lax.axis_index("replica")
    index = lax.axis_index("fsdp")
    core = lax.rem(index, 2)
    xc = lax.rem(index // 2, 4)
    zh = lax.rem(index // 8, 2)
    yc = index // 16

    def fsdp_of(y, h, x):
        return ((y * 2 + h) * 4 + x) * 2 + core

    def mod4(v):
        return lax.rem(v + 8, 4)

    partner = (zl, index + 1 - 2 * core)
    x_side = [(zl, fsdp_of(yc, zh, mod4(xc + d))) for d in (1, -1)]
    y_side = [(zl, fsdp_of(mod4(yc + d), zh, xc)) for d in (1, -1)]
    z_now = zh * 4 + zl

    def z_plus(k):
        return lax.rem(z_now + k + 8, 8)

    def z_dev(z):
        return (lax.rem(z, 4), fsdp_of(yc, z // 4, xc))

    z_peers = [z_dev(z_plus(k)) for k in range(1, 8)]
    z_side = [z_dev(z_plus(1)), z_dev(z_plus(-1))]
    mirror = z_dev(7 - z_now)

    barrier = pltpu.get_barrier_semaphore()
    for dev in [partner] + x_side + y_side + z_peers:
        pl.semaphore_signal(barrier, inc=1, device_id=dev, device_id_type=MESH)

    def place(t):
        h = lax.rem(1 - zh + t // 16, 2)
        return lax.rem(t // 4, 4), h, lax.rem(t, 4)

    def tok_cols(t, side):
        y, h, x = place(t)
        src = pl.multiple_of((2 * ((y * 2 + h) * 4 + x) + side) * 128, 128)
        dst = pl.multiple_of((h * 4 + x) * 128, 128)
        return y, src, dst

    def local_tok(t):
        y, src, dst = tok_cols(t, core)
        return pltpu.make_async_copy(
            tokens.at[:, pl.ds(src, 128)], tok.at[y, 0, :, pl.ds(dst, 128)], tok_local.at[t]
        )

    def remote_tok(t):
        y, src, dst = tok_cols(t, 1 - core)
        return pltpu.make_async_remote_copy(
            src_ref=tokens.at[:, pl.ds(src, 128)],
            dst_ref=tok.at[y, 1, :, pl.ds(dst, 128)],
            send_sem=tok_send.at[t],
            recv_sem=tok_recv.at[t],
            device_id=partner,
            device_id_type=MESH,
        )

    z_in = pltpu.make_async_copy(z_hbm, z_ref, in_sem.at[0])
    x_in = pltpu.make_async_copy(x_hbm, x_ref, in_sem.at[1])
    cot_local = pltpu.make_async_copy(cot_hbm, cot.at[0], in_sem.at[2])
    z_in.start()
    x_in.start()
    cot_local.start()

    @pl.loop(0, 32)
    def _(t):
        local_tok(t).start()

    z_in.wait()
    x_in.wait()
    blended = (1.0 - beta_first) * z_ref[...] + beta_first * x_ref[...]
    wts[yc, zh, xc] = blended.astype(BF16)

    pl.semaphore_wait(barrier, 12)

    sends = []
    counter = [0]

    def message(src, dst, dev):
        m = counter[0]
        counter[0] += 1
        copy = pltpu.make_async_remote_copy(
            src_ref=src, dst_ref=dst, send_sem=send_sem.at[m], recv_sem=recv_sem.at[m],
            device_id=dev, device_id_type=MESH,
        )
        copy.start()
        sends.append(copy)
        return m

    def arrived(m, dst):
        pltpu.make_async_remote_copy(
            src_ref=dst, dst_ref=dst, send_sem=send_sem.at[m], recv_sem=recv_sem.at[m],
            device_id=partner, device_id_type=MESH,
        ).wait_recv()

    first = (xc, yc)
    second = (yc, xc)
    first_side = (x_side, y_side)
    second_side = (y_side, x_side)

    def block(p, f, s, h, r0, rows):
        y, x = (s, f) if p == 0 else (f, s)
        return wts.at[y, h, x, pl.ds(r0, rows), :]

    half_of = (zh, 1 - zh)
    ag = {}

    def spread(st, p, item):
        h = half_of[st]
        blk = block(p, mod4(first[p] + item), second[p], h, 64 * p, 64)
        for d in (0, 1):
            ag[st, p, 2, item, d] = message(blk, blk, second_side[p][d])

    def ag0(st):
        h = half_of[st]
        for p in (0, 1):
            own = block(p, first[p], second[p], h, 64 * p, 64)
            for d in (0, 1):
                ag[st, p, 0, d] = message(own, own, first_side[p][d])
        for p in (0, 1):
            spread(st, p, 0)

    def ag1(st):
        h = half_of[st]
        for p in (0, 1):
            f, s, r0 = first[p], second[p], 64 * p
            for d in (0, 1):
                src_f = mod4(f - 1 + 2 * d)
                arrived(ag[st, p, 0, d], block(p, src_f, s, h, r0, 64))
                part = block(p, src_f, s, h, r0 + 32 * d, 32)
                ag[st, p, 1, d] = message(part, part, first_side[p][d])
                spread(st, p, -1 + 2 * d)

    def ag2(st):
        h = half_of[st]
        for p in (0, 1):
            f, s, r0 = first[p], second[p], 64 * p
            for d in (0, 1):
                arrived(ag[st, p, 1, d], block(p, mod4(f + 2), s, h, r0 + 32 * d, 32))
            spread(st, p, 2)

    def ag3(st, items):
        h = half_of[st]
        for item in items:
            for p in (0, 1):
                f, s, r0 = first[p], second[p], 64 * p
                for d in (0, 1):
                    src_s = mod4(s - 1 + 2 * d)
                    arrived(ag[st, p, 2, item, d], block(p, mod4(f + item), src_s, h, r0, 64))
                    part = block(p, mod4(f + item), src_s, h, r0 + 32 * d, 32)
                    ag[st, p, 3, item, d] = message(part, part, second_side[p][d])

    def ag4(st):
        h = half_of[st]
        for item in (0, -1, 1, 2):
            for p in (0, 1):
                f, s, r0 = first[p], second[p], 64 * p
                for d in (0, 1):
                    arrived(ag[st, p, 3, item, d], block(p, mod4(f + item), mod4(s + 2), h, r0 + 32 * d, 32))

    zc = {}

    def piece(z, c, r0, rows):
        row = pl.multiple_of(lax.rem(z, 4) * 64 + r0, 32)
        return gt.at[pl.ds(2 * c, 2), z // 4, :, pl.ds(row, rows), :]

    def zc1(c):
        dest = z_plus(4)
        for d in (0, 1):
            zc[1, d, c] = message(piece(dest, c, 32 * d, 32), zc_half.at[d, c], z_side[d])

    def zc_step(s, c):
        for d in (0, 1):
            dest = z_plus((5 - s) * (1 - 2 * d))
            h = dest // 4
            row = pl.multiple_of(lax.rem(dest, 4) * 64, 64)
            if s == 2:
                arrived(zc[1, d, c], zc_half.at[d, c])
            else:
                arrived(zc[s - 1, d, c], zc_recv.at[s - 3, d, c])

            @pl.loop(0, 8)
            def _(i):
                y, x = i // 4, lax.rem(i, 4)
                mine = gt[2 * c + y, h, x, pl.ds(row, 64), :]
                if s == 2:
                    a, b = 32 * d, 32 - 32 * d
                    got = zc_half[d, c, y, x].astype(F32)
                    zc_stage[0, d, c, y, x, a:a + 32, :] = (mine[a:a + 32, :].astype(F32) + got).astype(BF16)
                    zc_stage[0, d, c, y, x, b:b + 32, :] = mine[b:b + 32, :]
                else:
                    got = zc_recv[s - 3, d, c, y, x].astype(F32)
                    zc_stage[s - 2, d, c, y, x] = (mine.astype(F32) + got).astype(BF16)

            zc[s, d, c] = message(zc_stage.at[s - 2, d, c], zc_recv.at[s - 2, d, c], z_side[d])

    def zc_final(c):
        for d in (0, 1):
            arrived(zc[4, d, c], zc_recv.at[2, d, c])
        row = pl.multiple_of(zl * 64, 64)

        @pl.loop(0, 8)
        def _(i):
            y, x = i // 4, lax.rem(i, 4)
            total = (
                gt[2 * c + y, zh, x, pl.ds(row, 64), :].astype(F32)
                + zc_recv[2, 0, c, y, x].astype(F32)
                + zc_recv[2, 1, c, y, x].astype(F32)
            )
            for p in (0, 1):
                for k in (0, 1):
                    part = total[32 * p + 16 * k:32 * p + 16 * k + 16, :]
                    c_f[p, 2 * c + y, k, x] = part
                    c_b[p, 2 * c + y, k, x] = part.astype(BF16)

    def nxt(c, d):
        return mod4(c + 1 - 2 * d)

    class Plane:
        def __init__(self, pick, load, bufs):
            self.pick, self.load, self.bufs, self.m = pick, load, bufs, {}

        def start(self, p, which):
            rel, dirc = self.bufs[0], self.bufs[1]
            for d in (0, 1):
                if which == 0:
                    src, dst = self.pick(p, mod4(first[p] + 2), d), rel.at[p, d]
                else:
                    src, dst = self.pick(p, nxt(first[p], d), 1 - d), dirc.at[p, d]
                self.m[p, which, d] = message(src, dst, first_side[p][d])

        def mid(self, p):
            rel, _, summed, stage = self.bufs[:4]
            for d in (0, 1):
                arrived(self.m[p, 0, d], rel.at[p, d])

                @pl.loop(0, 4)
                def _(i):
                    stage[p, d, i] = (self.load(p, nxt(first[p], d), d, i) + rel[p, d, i].astype(F32)).astype(BF16)

                self.m[p, 2, d] = message(stage.at[p, d], summed.at[p, d], first_side[p][d])

        def turn(self, p):
            _, dirc, summed, _, gf, gb, rel2, dir2 = self.bufs[:8]
            for d in (0, 1):
                arrived(self.m[p, 1, d], dirc.at[p, d])
                arrived(self.m[p, 2, d], summed.at[p, d])
            for h in (0, 1):
                @pl.loop(0, 4)
                def _(i):
                    total = (
                        self.load(p, first[p], h, i)
                        + dirc[p, 1 - h, i].astype(F32)
                        + summed[p, h, i].astype(F32)
                    )
                    gf[p, i, h] = total
                    gb[p, i, h] = total.astype(BF16)
            s = second[p]
            for d in (0, 1):
                self.m[p, 3, d] = message(gb.at[p, mod4(s + 2), d], rel2.at[p, d], second_side[p][d])
            for d in (0, 1):
                self.m[p, 4, d] = message(gb.at[p, nxt(s, d), 1 - d], dir2.at[p, d], second_side[p][d])

        def mid2(self, p):
            gf, _, rel2, _, summed2, stage2_ = self.bufs[4:]
            for d in (0, 1):
                arrived(self.m[p, 3, d], rel2.at[p, d])
                stage2_[p, d] = (gf[p, nxt(second[p], d), d] + rel2[p, d].astype(F32)).astype(BF16)
                self.m[p, 5, d] = message(stage2_.at[p, d], summed2.at[p, d], second_side[p][d])

        def end(self, p):
            gf, _, _, dir2, summed2, _ = self.bufs[4:]
            for d in (0, 1):
                arrived(self.m[p, 4, d], dir2.at[p, d])
                arrived(self.m[p, 5, d], summed2.at[p, d])
            return [
                gf[p, second[p], h] + dir2[p, 1 - h].astype(F32) + summed2[p, h].astype(F32)
                for h in (0, 1)
            ]

    def ab_pick(p, f, h):
        rows = pl.ds(256 + 128 * p, 128)
        return gt.at[:, h, f, rows, :] if p == 0 else gt.at[f, h, :, rows, :]

    def ab_load(p, f, h, i):
        rows = pl.ds(256 + 128 * p, 128)
        return (gt[i, h, f, rows, :] if p == 0 else gt[f, h, i, rows, :]).astype(F32)

    def c_pick(p, f, h):
        return c_b.at[0, :, h, f] if p == 0 else c_b.at[1, f, h]

    def c_load(p, f, h, i):
        return c_f[0, i, h, f] if p == 0 else c_f[1, f, h, i]

    ab = Plane(ab_pick, ab_load, (relay1, direct1, summed1, stage1, g1f, g1b, relay2, direct2, summed2, stage2))
    cc = Plane(
        c_pick, c_load,
        (c_relay1, c_direct1, c_summed1, c_stage1, c_g1f, c_g1b, c_relay2, c_direct2, c_summed2, c_stage2),
    )

    def grad(j0, j1):
        @pl.loop(j0, j1)
        def _(j):
            for t in (2 * j, 2 * j + 1):
                local_tok(t).wait()
                remote_tok(t).wait_recv()
            y, h, x = place(2 * j)
            col = pl.multiple_of(h * 512 + x * 128, 256)
            rhs = tok[y, :, :, pl.ds(col, 256)].reshape(1024, 256)
            for q in (0, 1):
                rows = slice(256 * q, 256 * (q + 1))
                out = jnp.dot(cot_t[rows, :], rhs, preferred_element_type=F32).astype(BF16)
                gt[y, h, x, rows, :] = out[:, :128]
                gt[y, h, x + 1, rows, :] = out[:, 128:]

    def values(y):
        @pl.loop(0, 2)
        def _(m):
            out = jnp.dot(tok[y, m], wts[y].reshape(1024, 512), preferred_element_type=F32)
            acc[m] = out if y == 0 else acc[m] + out

    cot_msg = message(cot_hbm, cot.at[1], partner)
    ag0(0)
    own = wts.at[yc, zh, xc]
    mirror_msg = message(own, own, mirror)

    @pl.loop(0, 32)
    def _(t):
        remote_tok(t).start()

    cot_local.wait()
    arrived(cot_msg, cot.at[1])
    for k in (0, 1):
        cot_t[:, 512 * k:512 * (k + 1)] = cot[k].T

    ag1(0)
    grad(0, 2)
    ag2(0)
    grad(2, 4)
    zc1(0)
    arrived(mirror_msg, wts.at[yc, 1 - zh, xc])
    ag0(1)
    grad(4, 6)
    ag3(0, (0,))
    grad(6, 8)
    zc1(1)
    ag1(1)
    grad(8, 12)
    ag3(0, (-1, 1))
    ag2(1)
    grad(12, 16)
    zc_step(2, 0)
    for p in (0, 1):
        ab.start(p, 0)
    ag3(0, (2,))
    ag3(1, (0,))
    zc_step(2, 1)
    ag3(1, (-1, 1))
    zc_step(3, 0)
    for p in (0, 1):
        ab.start(p, 1)
    ag3(1, (2,))
    ag4(0)
    zc_step(3, 1)
    for p in (0, 1):
        ab.mid(p)
    zc_step(4, 0)
    ag4(1)
    values(0)
    zc_step(4, 1)
    values(1)
    for p in (0, 1):
        ab.turn(p)
    zc_final(0)
    zc_final(1)
    for p in (0, 1):
        cc.start(p, 0)
        cc.start(p, 1)
    values(2)
    for p in (0, 1):
        ab.mid2(p)
        cc.mid(p)
    values(3)
    vmsg = message(acc.at[1], vrecv, partner)
    for p in (0, 1):
        cc.turn(p)
    for p in (0, 1):
        for h, total in enumerate(ab.end(p)):
            plane[h, 128 * p:128 * (p + 1), :] = total
            zstage[h, 128 * p:128 * (p + 1), :] = total.astype(BF16)

    zmsgs = []
    for k in range(1, 8):
        dest = z_plus(k)
        part = zstage.at[dest // 4, pl.ds(pl.multiple_of(lax.rem(dest, 4) * 64, 64), 64), :]
        zmsgs.append(message(part, zrecv.at[k - 1], z_peers[k - 1]))

    for p in (0, 1):
        cc.mid2(p)

    def share(base):
        rows = gfull.at[pl.ds(pl.multiple_of(base + zl * 64, 64), 64), :]
        return [message(rows, rows, (lax.rem(zl + k, 4), index)) for k in range(1, 4)]

    def shared(base, msgs):
        for k in range(1, 4):
            row = pl.multiple_of(base + lax.rem(zl + 4 - k, 4) * 64, 64)
            arrived(msgs[k - 1], gfull.at[pl.ds(row, 64), :])

    my_rows = pl.ds(pl.multiple_of(zl * 64, 64), 64)
    for p in (0, 1):
        for h, total in enumerate(cc.end(p)):
            gfull[pl.ds(pl.multiple_of(zl * 64 + 32 * p + 16 * h, 16), 16), :] = total
    c_msgs = share(0)

    total = plane[zh, my_rows, :]
    for k in range(7):
        arrived(zmsgs[k], zrecv.at[k])
        total = total + zrecv[k].astype(F32)
    gfull[pl.ds(pl.multiple_of(256 + zl * 64, 64), 64), :] = total
    ab_msgs = share(256)

    arrived(vmsg, vrecv)
    values_out[...] = ((acc[0] + vrecv[...]) * NORM).astype(BF16)

    shared(0, c_msgs)
    shared(256, ab_msgs)
    grad_out[...] = gfull[...]

    for copy in sends:
        copy.wait_send()

    @pl.loop(0, 32)
    def _(t):
        remote_tok(t).wait_send()

    assert counter[0] <= N_MSG


def finish(values_ref, grad_ref, z_ref, x_ref, s_ref, values_out, z_out, x_out, s_out):
    values_out[...] = values_ref[...]
    gradient = grad_ref[...].T * NORM
    z_in = z_ref[...]
    x_in = x_ref[...]
    mixed = (1.0 - beta_first) * z_in + beta_first * x_in
    second_next = beta_second * s_ref[...] + (1.0 - beta_second) * gradient * gradient
    scaled = gradient / (jnp.sqrt(second_next / bias_fix) + epsilon)
    z_next = z_in - learn_rate * (scaled + weight_decay * mixed)
    s_out[...] = second_next
    z_out[...] = z_next
    x_out[...] = (1.0 - mixing) * x_in + mixing * z_next


def local(tokens, cotangent, z_weights, x_weights, second_moment):
    vm = pl.BlockSpec(memory_space=pltpu.VMEM)
    hbm = pl.BlockSpec(memory_space=pl.ANY)
    shard = jax.ShapeDtypeStruct((128, HV), F32)
    vals = jax.ShapeDtypeStruct((TOK, HV), BF16)
    dma = pltpu.SemaphoreType.DMA

    def plane_bufs(r):
        return (
            [pltpu.VMEM((2, 2, 4, r, 128), BF16)] * 4
            + [pltpu.VMEM((2, 4, 2, r, 128), F32), pltpu.VMEM((2, 4, 2, r, 128), BF16)]
            + [pltpu.VMEM((2, 2, r, 128), BF16)] * 4
        )

    values, gradient = pl.pallas_call(
        kernel,
        out_shape=(vals, jax.ShapeDtypeStruct((HV, 128), F32)),
        in_specs=[hbm, hbm, hbm, hbm],
        out_specs=(vm, vm),
        scratch_shapes=[
            pltpu.VMEM((128, HV), F32),
            pltpu.VMEM((128, HV), F32),
            pltpu.VMEM((4, 2, 512, 1024), BF16),
            pltpu.VMEM((2, 512, 512), BF16),
            pltpu.VMEM((512, 1024), BF16),
            pltpu.VMEM((4, 2, 4, 128, 512), BF16),
            pltpu.VMEM((4, 2, 4, 512, 128), BF16),
        ] + plane_bufs(128) + [
            pltpu.VMEM((2, 4, 2, 4, 16, 128), F32),
            pltpu.VMEM((2, 4, 2, 4, 16, 128), BF16),
        ] + plane_bufs(16) + [
            pltpu.VMEM((2, 2, 2, 4, 32, 128), BF16),
            pltpu.VMEM((3, 2, 2, 2, 4, 64, 128), BF16),
            pltpu.VMEM((3, 2, 2, 2, 4, 64, 128), BF16),
            pltpu.VMEM((2, 256, 128), F32),
            pltpu.VMEM((2, 256, 128), BF16),
            pltpu.VMEM((7, 64, 128), BF16),
            pltpu.VMEM((512, 128), F32),
            pltpu.VMEM((2, 512, 512), F32),
            pltpu.VMEM((512, 512), F32),
            dma((N_MSG,)),
            dma((N_MSG,)),
            dma((32,)),
            dma((32,)),
            dma((32,)),
            dma((3,)),
        ],
        compiler_params=pltpu.CompilerParams(
            collective_id=0, has_side_effects=True, vmem_limit_bytes=48 * 1024 * 1024
        ),
    )(tokens, cotangent, z_weights, x_weights)
    return pl.pallas_call(
        finish,
        out_shape=(vals, shard, shard, shard),
        in_specs=[vm] * 5,
        out_specs=(vm,) * 4,
        compiler_params=pltpu.CompilerParams(vmem_limit_bytes=12 * 1024 * 1024),
    )(values, gradient, z_weights, x_weights, second_moment)


def solution(mesh):
    return jax.shard_map(
        local,
        mesh=mesh,
        in_specs=(
            P(("replica", "fsdp"), None),
            P(("replica", "fsdp"), None),
            P("fsdp", None),
            P("fsdp", None),
            P("fsdp", None),
        ),
        out_specs=(P(("replica", "fsdp"), None), P("fsdp", None), P("fsdp", None), P("fsdp", None)),
        check_vma=False,
    )
```

time: 654 us -> 77.9 us (0.12)
  waiting for transfers between devices: 610 us -> 0 us
  Pallas kernels: 0 us -> 74 us
  matrix products: 22 us -> 0 us
  between operations: 13.8 us -> 0.66 us
    reduce_scatter x1 -> x0, waiting for transfers between devices: 446 us -> none  [local(): lax.psum_scatter(jnp.einsum('td,th->dh', columns, cotangent, preferred_el...]
    all_gather x1 -> x0, waiting for transfers between devices: 116 us -> none  [local(): lax.all_gather(weights, 'fsdp', axis=0, tiled=True)]
    pallas_call x0 -> x2, Pallas kernels: none -> 74 us  [the longest x1 72.7 us: local(): pl.pallas_call(kernel, out_shape=(vals, jax.ShapeDtypeStruct((HV, 128), F...]
    psum x1 -> x0, waiting for transfers between devices: 47.8 us -> none  [local(): lax.psum(partial_sum.astype(jnp.bfloat16), 'replica').astype(jnp.float32)]
    dot_general x2 -> x0, matrix products: 22 us -> none  [the longest x1 11.7 us: local(): jnp.einsum('td,th->dh', columns, cotangent, preferred_element_type=jnp.fl...]
  transfers between devices with their start and end apart: 3 -> 0, of which waited for: 3 -> 0; matrix products, arithmetic and copies ran while one was open for 0% -> 0% of each run, Pallas kernels for 0% -> 0%
where the time goes in v2:
time: 77.9 us; the launch traced here: 77.6 us
  Pallas kernels  74 us (95%)
  local copies, waits for them, and re-layouts  2.94 us (4%)
    pallas_call x1, Pallas kernels, local(): pl.pallas_call(kernel, out_shape=(vals, jax.ShapeDtypeStruct((HV, 128), F...  72.7 us
    unnamed x8, local copies, waits for them, and re-layouts  2.94 us

profile of v2, /device:TPU:32, one launch (start us, length us, event | category | flops | bytes accessed | tf_op | source)
XLA Modules:
  0.0 77.6 jit_solution(12068508859041800916)
XLA Ops:
  0.6 0.0 copy-start
  0.6 0.9 %copy-done = f32[128,512]{1,0:T(8,128)S(1)} copy-done((f32[128,512]{1,0:T(8,128)S(1)}, f32[128,512]{1,0:T(8,128)}, u32[]{:S(2)}) %copy-start) | copy-done | bytes 262168
  1.6 0.0 copy-start.1
  1.6 0.9 %copy-done.1 = f32[128,512]{1,0:T(8,128)S(1)} copy-done((f32[128,512]{1,0:T(8,128)S(1)}, f32[128,512]{1,0:T(8,128)}, u32[]{:S(2)}) %copy-start.1) | copy-done | bytes 262168
  2.5 0.0 copy-start.2
  2.5 1.0 %copy-done.2 = bf16[512,512]{1,0:T(8,128)(2,1)S(1)} copy-done((bf16[512,512]{1,0:T(8,128)(2,1)S(1)}, bf16[512,512]{1,0:T(8,128)(2,1)}, u32[]{:S(2)}) %copy-start.2) | copy-done | bytes 524312
  3.6 0.0 copy-start.3
  3.6 72.7 %shard_map.84 = (bf16[512,512]{1,0:T(8,128)(2,1)S(1)}, f32[512,128]{1,0:T(8,128)S(1)}) custom-call(bf16[512,8192]{1,0:T(8,128)(2,1)} %tokens.1, bf16[512,512]{1,0:T(8,128)(2,1)S(1)} %copy-done.2, f32[128,512]{1,0:T(8,128)S(1)} %copy-done, f32[128,512]{1,0:T(8,128)S(1)} %copy-done.1), custom_call_target="tpu_custom_call" | custom-call | tf_op jit(solution)/shard_map/pallas_call | solution.py:509
  76.3 0.0 copy-done.3
  76.3 1.3 %shard_map.85 = (bf16[512,512]{1,0:T(8,128)(2,1)}, f32[128,512]{1,0:T(8,128)}, f32[128,512]{1,0:T(8,128)}, f32[128,512]{1,0:T(8,128)}) custom-call(bf16[512,512]{1,0:T(8,128)(2,1)S(1)} %get-tuple-element.6.values_ref, f32[512,128]{1,0:T(8,128)S(1)} %get-tuple-element.7.grad_ref, f32[128,512]{1,0:T(8,128)S(1)} %copy-done, f32[128,512]{1,0:T(8,128)S(1)} %copy-done.1, ...), custom_call_target="tpu_custom_call" | custom-call | tf_op jit(solution)/shard_map/pallas_call | solution.py:546
Async XLA Ops:
  0.6 1.0 %copy-start = (f32[128,512]{1,0:T(8,128)S(1)}, f32[128,512]{1,0:T(8,128)}, u32[]{:S(2)}) copy-start(f32[128,512]{1,0:T(8,128)} %z_ref.1) | copy-start | bytes 786436
  1.6 0.9 %copy-start.1 = (f32[128,512]{1,0:T(8,128)S(1)}, f32[128,512]{1,0:T(8,128)}, u32[]{:S(2)}) copy-start(f32[128,512]{1,0:T(8,128)} %x_ref.1) | copy-start | bytes 786436
  2.5 1.0 %copy-start.2 = (bf16[512,512]{1,0:T(8,128)(2,1)S(1)}, bf16[512,512]{1,0:T(8,128)(2,1)}, u32[]{:S(2)}) copy-start(bf16[512,512]{1,0:T(8,128)(2,1)} %cot_hbm.1) | copy-start | bytes 1572868
  3.6 72.7 %copy-start.3 = (f32[128,512]{1,0:T(8,128)S(1)}, f32[128,512]{1,0:T(8,128)}, u32[]{:S(2)}) copy-start(f32[128,512]{1,0:T(8,128)} %s_ref.1) | copy-start | bytes 786436

commit v3 on v2

--- a/solution.py
+++ b/solution.py
@@ -23,7 +23,11 @@
 F32 = jnp.float32
 BF16 = jnp.bfloat16
 MESH = pl.DeviceIdType.MESH
-N_MSG = 176
+N_MSG = 160
+C_ROWS = 80
+AB = 4 * C_ROWS
+R = (HV - AB) // 2
+Q = R // 2
 
 
 def kernel(
@@ -31,8 +35,7 @@
     values_out, grad_out,
     z_ref, x_ref, tok, cot, cot_t, wts, gt,
     relay1, direct1, summed1, stage1, g1f, g1b, relay2, direct2, summed2, stage2,
-    c_f, c_b,
-    c_relay1, c_direct1, c_summed1, c_stage1, c_g1f, c_g1b, c_relay2, c_direct2, c_summed2, c_stage2,
+    c_f, c_b, c_recv,
     zc_half, zc_recv, zc_stage,
     plane, zstage, zrecv, gfull, acc, vrecv,
     send_sem, recv_sem, tok_local, tok_send, tok_recv, in_sem,
@@ -65,8 +68,21 @@
     z_side = [z_dev(z_plus(1)), z_dev(z_plus(-1))]
     mirror = z_dev(7 - z_now)
 
+    def plane_plus(k):
+        return lax.rem(yc * 4 + xc + k, 16)
+
+    def plane_dev(i):
+        return (zl, fsdp_of(i // 4, zh, lax.rem(i, 4)))
+
+    plane_peers = [plane_dev(plane_plus(k)) for k in range(1, 16)]
+
+    z_in = pltpu.make_async_copy(z_hbm, z_ref, in_sem.at[0])
+    x_in = pltpu.make_async_copy(x_hbm, x_ref, in_sem.at[1])
+    z_in.start()
+    x_in.start()
+
     barrier = pltpu.get_barrier_semaphore()
-    for dev in [partner] + x_side + y_side + z_peers:
+    for dev in [partner] + plane_peers + z_peers:
         pl.semaphore_signal(barrier, inc=1, device_id=dev, device_id_type=MESH)
 
     def place(t):
@@ -96,11 +112,7 @@
             device_id_type=MESH,
         )
 
-    z_in = pltpu.make_async_copy(z_hbm, z_ref, in_sem.at[0])
-    x_in = pltpu.make_async_copy(x_hbm, x_ref, in_sem.at[1])
     cot_local = pltpu.make_async_copy(cot_hbm, cot.at[0], in_sem.at[2])
-    z_in.start()
-    x_in.start()
     cot_local.start()
 
     @pl.loop(0, 32)
@@ -112,7 +124,7 @@
     blended = (1.0 - beta_first) * z_ref[...] + beta_first * x_ref[...]
     wts[yc, zh, xc] = blended.astype(BF16)
 
-    pl.semaphore_wait(barrier, 12)
+    pl.semaphore_wait(barrier, 23)
 
     sends = []
     counter = [0]
@@ -201,58 +213,71 @@
 
     zc = {}
 
-    def piece(z, c, r0, rows):
-        row = pl.multiple_of(lax.rem(z, 4) * 64 + r0, 32)
-        return gt.at[pl.ds(2 * c, 2), z // 4, :, pl.ds(row, rows), :]
+    def c_row(z):
+        return pl.multiple_of(lax.rem(z, 4) * C_ROWS, 16)
 
     def zc1(c):
         dest = z_plus(4)
         for d in (0, 1):
-            zc[1, d, c] = message(piece(dest, c, 32 * d, 32), zc_half.at[d, c], z_side[d])
+            half = gt.at[pl.ds(2 * c, 2), dest // 4, pl.ds(2 * d, 2), pl.ds(c_row(dest), C_ROWS), :]
+            zc[1, d, c] = message(half, zc_half.at[d, c], z_side[d])
 
     def zc_step(s, c):
         for d in (0, 1):
             dest = z_plus((5 - s) * (1 - 2 * d))
-            h = dest // 4
-            row = pl.multiple_of(lax.rem(dest, 4) * 64, 64)
+            h, row = dest // 4, c_row(dest)
             if s == 2:
                 arrived(zc[1, d, c], zc_half.at[d, c])
+
+                @pl.loop(0, 4)
+                def _(i):
+                    y, x = i // 2, lax.rem(i, 2)
+                    mine = gt[2 * c + y, h, 2 * d + x, pl.ds(row, C_ROWS), :].astype(F32)
+                    got = zc_half[d, c, y, x].astype(F32)
+                    zc_stage[0, d, c, y, 2 * d + x] = (mine + got).astype(BF16)
+                    other = 2 * (1 - d) + x
+                    zc_stage[0, d, c, y, other] = gt[2 * c + y, h, other, pl.ds(row, C_ROWS), :]
             else:
                 arrived(zc[s - 1, d, c], zc_recv.at[s - 3, d, c])
 
-            @pl.loop(0, 8)
-            def _(i):
-                y, x = i // 4, lax.rem(i, 4)
-                mine = gt[2 * c + y, h, x, pl.ds(row, 64), :]
-                if s == 2:
-                    a, b = 32 * d, 32 - 32 * d
-                    got = zc_half[d, c, y, x].astype(F32)
-                    zc_stage[0, d, c, y, x, a:a + 32, :] = (mine[a:a + 32, :].astype(F32) + got).astype(BF16)
-                    zc_stage[0, d, c, y, x, b:b + 32, :] = mine[b:b + 32, :]
-                else:
+                @pl.loop(0, 8)
+                def _(i):
+                    y, x = i // 4, lax.rem(i, 4)
+                    mine = gt[2 * c + y, h, x, pl.ds(row, C_ROWS), :].astype(F32)
                     got = zc_recv[s - 3, d, c, y, x].astype(F32)
-                    zc_stage[s - 2, d, c, y, x] = (mine.astype(F32) + got).astype(BF16)
+                    zc_stage[s - 2, d, c, y, x] = (mine + got).astype(BF16)
 
             zc[s, d, c] = message(zc_stage.at[s - 2, d, c], zc_recv.at[s - 2, d, c], z_side[d])
 
     def zc_final(c):
         for d in (0, 1):
             arrived(zc[4, d, c], zc_recv.at[2, d, c])
-        row = pl.multiple_of(zl * 64, 64)
+        row = c_row(z_now)
 
         @pl.loop(0, 8)
         def _(i):
             y, x = i // 4, lax.rem(i, 4)
             total = (
-                gt[2 * c + y, zh, x, pl.ds(row, 64), :].astype(F32)
+                gt[2 * c + y, zh, x, pl.ds(row, C_ROWS), :].astype(F32)
                 + zc_recv[2, 0, c, y, x].astype(F32)
                 + zc_recv[2, 1, c, y, x].astype(F32)
             )
-            for p in (0, 1):
-                for k in (0, 1):
-                    part = total[32 * p + 16 * k:32 * p + 16 * k + 16, :]
-                    c_f[p, 2 * c + y, k, x] = part
-                    c_b[p, 2 * c + y, k, x] = part.astype(BF16)
+            c_f[2 * c + y, x] = total
+            c_b[2 * c + y, x] = total.astype(BF16)
+
+    def c_send():
+        out = []
+        for k in range(1, 16):
+            i = plane_plus(k)
+            out.append(message(c_b.at[i // 4, lax.rem(i, 4)], c_recv.at[k - 1], plane_peers[k - 1]))
+        return out
+
+    def c_end(msgs):
+        total = c_f[yc, xc]
+        for k in range(15):
+            arrived(msgs[k], c_recv.at[k])
+            total = total + c_recv[k].astype(F32)
+        gfull[pl.ds(c_row(z_now), C_ROWS), :] = total
 
     def nxt(c, d):
         return mod4(c + 1 - 2 * d)
@@ -320,24 +345,14 @@
             ]
 
     def ab_pick(p, f, h):
-        rows = pl.ds(256 + 128 * p, 128)
+        rows = pl.ds(AB + R * p, R)
         return gt.at[:, h, f, rows, :] if p == 0 else gt.at[f, h, :, rows, :]
 
     def ab_load(p, f, h, i):
-        rows = pl.ds(256 + 128 * p, 128)
+        rows = pl.ds(AB + R * p, R)
         return (gt[i, h, f, rows, :] if p == 0 else gt[f, h, i, rows, :]).astype(F32)
 
-    def c_pick(p, f, h):
-        return c_b.at[0, :, h, f] if p == 0 else c_b.at[1, f, h]
-
-    def c_load(p, f, h, i):
-        return c_f[0, i, h, f] if p == 0 else c_f[1, f, h, i]
-
     ab = Plane(ab_pick, ab_load, (relay1, direct1, summed1, stage1, g1f, g1b, relay2, direct2, summed2, stage2))
-    cc = Plane(
-        c_pick, c_load,
-        (c_relay1, c_direct1, c_summed1, c_stage1, c_g1f, c_g1b, c_relay2, c_direct2, c_summed2, c_stage2),
-    )
 
     def grad(j0, j1):
         @pl.loop(j0, j1)
@@ -354,118 +369,128 @@
                 gt[y, h, x, rows, :] = out[:, :128]
                 gt[y, h, x + 1, rows, :] = out[:, 128:]
 
-    def values(y):
-        @pl.loop(0, 2)
-        def _(m):
-            out = jnp.dot(tok[y, m], wts[y].reshape(1024, 512), preferred_element_type=F32)
-            acc[m] = out if y == 0 else acc[m] + out
+    def values(st, y, m):
+        h = half_of[st]
+        lhs = tok[y, m, :, pl.ds(pl.multiple_of(h * 512, 512), 512)]
+        out = jnp.dot(lhs, wts[y, h].reshape(512, 512), preferred_element_type=F32)
+        acc[m] = out if (st, y) == (0, 0) else acc[m] + out
+
+    def z_send():
+        out = []
+        for k in range(1, 8):
+            dest = z_plus(k)
+            part = zstage.at[dest // 4, pl.ds(pl.multiple_of(lax.rem(dest, 4) * Q, 16), Q), :]
+            out.append(message(part, zrecv.at[k - 1], z_peers[k - 1]))
+        return out
+
+    def z_end(msgs):
+        total = plane[zh, pl.ds(pl.multiple_of(zl * Q, 16), Q), :]
+        for k in range(7):
+            arrived(msgs[k], zrecv.at[k])
+            total = total + zrecv[k].astype(F32)
+        gfull[pl.ds(pl.multiple_of(AB + zl * Q, 16), Q), :] = total
+
+    def share(base, n):
+        rows = gfull.at[pl.ds(pl.multiple_of(base + zl * n, 16), n), :]
+        return [message(rows, rows, (lax.rem(zl + k, 4), index)) for k in range(1, 4)]
+
+    def shared(base, n, msgs):
+        for k in range(1, 4):
+            row = pl.multiple_of(base + lax.rem(zl + 4 - k, 4) * n, 16)
+            arrived(msgs[k - 1], gfull.at[pl.ds(row, n), :])
+
+    def ab_start(which):
+        for p in (0, 1):
+            ab.start(p, which)
+
+    def ab_all(step):
+        for p in (0, 1):
+            step(p)
+
+    def ab_end():
+        for p in (0, 1):
+            for h, total in enumerate(ab.end(p)):
+                plane[h, R * p:R * (p + 1), :] = total
+                zstage[h, R * p:R * (p + 1), :] = total.astype(BF16)
 
     cot_msg = message(cot_hbm, cot.at[1], partner)
     ag0(0)
-    own = wts.at[yc, zh, xc]
-    mirror_msg = message(own, own, mirror)
 
     @pl.loop(0, 32)
     def _(t):
         remote_tok(t).start()
 
+    own = wts.at[yc, zh, xc]
+    mirror_msg = message(own, own, mirror)
     cot_local.wait()
     arrived(cot_msg, cot.at[1])
     for k in (0, 1):
         cot_t[:, 512 * k:512 * (k + 1)] = cot[k].T
-
-    ag1(0)
     grad(0, 2)
-    ag2(0)
     grad(2, 4)
     zc1(0)
+    grad(4, 6)
+    grad(6, 8)
+    zc1(1)
+    ag1(0)
+    grad(8, 10)
+    grad(10, 12)
+    grad(12, 14)
+    grad(14, 16)
+    ab_start(0)
+    zc_step(2, 0)
+    ag2(0)
+    ag3(0, (0,))
+    ab_start(1)
     arrived(mirror_msg, wts.at[yc, 1 - zh, xc])
     ag0(1)
-    grad(4, 6)
-    ag3(0, (0,))
-    grad(6, 8)
-    zc1(1)
+    zc_step(2, 1)
+    ag3(0, (-1, 1))
+    zc_step(3, 0)
+    zc_step(3, 1)
+    ag3(0, (2,))
+    ab_all(ab.mid)
     ag1(1)
-    grad(8, 12)
-    ag3(0, (-1, 1))
+    ag3(1, (0,))
+    ag4(0)
+    values(0, 0, 0)
+    values(0, 0, 1)
+    values(0, 1, 0)
+    values(0, 1, 1)
+    values(0, 2, 0)
+    values(0, 2, 1)
+    zc_step(4, 0)
+    values(0, 3, 0)
+    values(0, 3, 1)
+    zc_step(4, 1)
     ag2(1)
-    grad(12, 16)
-    zc_step(2, 0)
-    for p in (0, 1):
-        ab.start(p, 0)
-    ag3(0, (2,))
-    ag3(1, (0,))
-    zc_step(2, 1)
+    ab_all(ab.turn)
     ag3(1, (-1, 1))
-    zc_step(3, 0)
-    for p in (0, 1):
-        ab.start(p, 1)
     ag3(1, (2,))
-    ag4(0)
-    zc_step(3, 1)
-    for p in (0, 1):
-        ab.mid(p)
-    zc_step(4, 0)
-    ag4(1)
-    values(0)
-    zc_step(4, 1)
-    values(1)
-    for p in (0, 1):
-        ab.turn(p)
+    ab_all(ab.mid2)
     zc_final(0)
     zc_final(1)
-    for p in (0, 1):
-        cc.start(p, 0)
-        cc.start(p, 1)
-    values(2)
-    for p in (0, 1):
-        ab.mid2(p)
-        cc.mid(p)
-    values(3)
+    ab_end()
+    z_msgs = z_send()
+    c_msgs = c_send()
+    ag4(1)
+    values(1, 0, 1)
+    values(1, 1, 1)
+    values(1, 2, 1)
+    values(1, 3, 1)
+    values(1, 0, 0)
+    values(1, 1, 0)
+    values(1, 2, 0)
+    values(1, 3, 0)
+    z_end(z_msgs)
+    ab_share = share(AB, Q)
     vmsg = message(acc.at[1], vrecv, partner)
-    for p in (0, 1):
-        cc.turn(p)
-    for p in (0, 1):
-        for h, total in enumerate(ab.end(p)):
-            plane[h, 128 * p:128 * (p + 1), :] = total
-            zstage[h, 128 * p:128 * (p + 1), :] = total.astype(BF16)
-
-    zmsgs = []
-    for k in range(1, 8):
-        dest = z_plus(k)
-        part = zstage.at[dest // 4, pl.ds(pl.multiple_of(lax.rem(dest, 4) * 64, 64), 64), :]
-        zmsgs.append(message(part, zrecv.at[k - 1], z_peers[k - 1]))
-
-    for p in (0, 1):
-        cc.mid2(p)
-
-    def share(base):
-        rows = gfull.at[pl.ds(pl.multiple_of(base + zl * 64, 64), 64), :]
-        return [message(rows, rows, (lax.rem(zl + k, 4), index)) for k in range(1, 4)]
-
-    def shared(base, msgs):
-        for k in range(1, 4):
-            row = pl.multiple_of(base + lax.rem(zl + 4 - k, 4) * 64, 64)
-            arrived(msgs[k - 1], gfull.at[pl.ds(row, 64), :])
-
-    my_rows = pl.ds(pl.multiple_of(zl * 64, 64), 64)
-    for p in (0, 1):
-        for h, total in enumerate(cc.end(p)):
-            gfull[pl.ds(pl.multiple_of(zl * 64 + 32 * p + 16 * h, 16), 16), :] = total
-    c_msgs = share(0)
-
-    total = plane[zh, my_rows, :]
-    for k in range(7):
-        arrived(zmsgs[k], zrecv.at[k])
-        total = total + zrecv[k].astype(F32)
-    gfull[pl.ds(pl.multiple_of(256 + zl * 64, 64), 64), :] = total
-    ab_msgs = share(256)
-
+    c_end(c_msgs)
+    c_share = share(0, C_ROWS)
     arrived(vmsg, vrecv)
     values_out[...] = ((acc[0] + vrecv[...]) * NORM).astype(BF16)
-
-    shared(0, c_msgs)
-    shared(256, ab_msgs)
+    shared(0, C_ROWS, c_share)
+    shared(AB, Q, ab_share)
     grad_out[...] = gfull[...]
 
     for copy in sends:
@@ -519,16 +544,16 @@
             pltpu.VMEM((512, 1024), BF16),
             pltpu.VMEM((4, 2, 4, 128, 512), BF16),
             pltpu.VMEM((4, 2, 4, 512, 128), BF16),
-        ] + plane_bufs(128) + [
-            pltpu.VMEM((2, 4, 2, 4, 16, 128), F32),
-            pltpu.VMEM((2, 4, 2, 4, 16, 128), BF16),
-        ] + plane_bufs(16) + [
-            pltpu.VMEM((2, 2, 2, 4, 32, 128), BF16),
-            pltpu.VMEM((3, 2, 2, 2, 4, 64, 128), BF16),
-            pltpu.VMEM((3, 2, 2, 2, 4, 64, 128), BF16),
-            pltpu.VMEM((2, 256, 128), F32),
-            pltpu.VMEM((2, 256, 128), BF16),
-            pltpu.VMEM((7, 64, 128), BF16),
+        ] + plane_bufs(R) + [
+            pltpu.VMEM((4, 4, C_ROWS, 128), F32),
+            pltpu.VMEM((4, 4, C_ROWS, 128), BF16),
+            pltpu.VMEM((15, C_ROWS, 128), BF16),
+            pltpu.VMEM((2, 2, 2, 2, C_ROWS, 128), BF16),
+            pltpu.VMEM((3, 2, 2, 2, 4, C_ROWS, 128), BF16),
+            pltpu.VMEM((3, 2, 2, 2, 4, C_ROWS, 128), BF16),
+            pltpu.VMEM((2, 2 * R, 128), F32),
+            pltpu.VMEM((2, 2 * R, 128), BF16),
+            pltpu.VMEM((7, Q, 128), BF16),
             pltpu.VMEM((512, 128), F32),
             pltpu.VMEM((2, 512, 512), F32),
             pltpu.VMEM((512, 512), F32),
@@ -542,7 +567,7 @@
         compiler_params=pltpu.CompilerParams(
             collective_id=0, has_side_effects=True, vmem_limit_bytes=48 * 1024 * 1024
         ),
-    )(tokens, cotangent, z_weights, x_weights)
+    )(tokens, *[pltpu.with_memory_space_constraint(a, pltpu.HBM) for a in (cotangent, z_weights, x_weights)])
     return pl.pallas_call(
         finish,
         out_shape=(vals, shard, shard, shard),

time: 77.9 us -> 63.9 us (0.82)
  Pallas kernels: 74 us -> 63.1 us
  local copies, waits for them, and re-layouts: 2.94 us -> 0.01 us
    pallas_call x1, Pallas kernels: 72.7 us -> 61.8 us  [local(): pl.pallas_call(kernel, out_shape=(vals, jax.ShapeDtypeStruct((HV, 128), F...]
    unnamed x8 -> x6, local copies, waits for them, and re-layouts: 2.94 us -> 0.01 us
where the time goes in v3:
time: 63.9 us; the launch traced here: 63.8 us
  Pallas kernels  63.1 us (99%)
  between operations  0.69 us (1%)
    pallas_call x1, Pallas kernels, local(): pl.pallas_call(kernel, out_shape=(vals, jax.ShapeDtypeStruct((HV, 128), F...  61.8 us
    pallas_call x1, Pallas kernels, local(): pl.pallas_call(finish, out_shape=(vals, shard, shard, shard), in_specs=[v...  1.34 us

profile of v3, /device:TPU:32, one launch (start us, length us, event | category | flops | bytes accessed | tf_op | source)
XLA Modules:
  0.0 63.8 jit_solution(2431990410257706229)
XLA Ops:
  0.6 0.0 copy-start.1
  0.6 0.0 copy-start
  0.7 0.0 copy-start.2
  0.7 61.8 %shard_map.84 = (bf16[512,512]{1,0:T(8,128)(2,1)S(1)}, f32[512,128]{1,0:T(8,128)S(1)}) custom-call(bf16[512,8192]{1,0:T(8,128)(2,1)} %tokens.1, bf16[512,512]{1,0:T(8,128)(2,1)} %cot_hbm.1, f32[128,512]{1,0:T(8,128)} %z_ref.1, f32[128,512]{1,0:T(8,128)} %x_ref.1), custom_call_target="tpu_custom_call" | custom-call | tf_op jit(solution)/shard_map/pallas_call | solution.py:534
  62.4 0.0 copy-done.1
  62.4 0.0 copy-done
  62.5 0.0 copy-done.2
  62.5 1.3 %shard_map.85 = (bf16[512,512]{1,0:T(8,128)(2,1)}, f32[128,512]{1,0:T(8,128)}, f32[128,512]{1,0:T(8,128)}, f32[128,512]{1,0:T(8,128)}) custom-call(bf16[512,512]{1,0:T(8,128)(2,1)S(1)} %get-tuple-element.6.values_ref, f32[512,128]{1,0:T(8,128)S(1)} %get-tuple-element.7.grad_ref, f32[128,512]{1,0:T(8,128)S(1)} %copy-done, f32[128,512]{1,0:T(8,128)S(1)} %copy-done.1, ...), custom_call_target="tpu_custom_call" | custom-call | tf_op jit(solution)/shard_map/pallas_call | solution.py:571
Async XLA Ops:
  0.6 61.8 %copy-start.1 = (f32[128,512]{1,0:T(8,128)S(1)}, f32[128,512]{1,0:T(8,128)}, u32[]{:S(2)}) copy-start(f32[128,512]{1,0:T(8,128)} %x_ref.1) | copy-start | bytes 786436
  0.6 61.8 %copy-start = (f32[128,512]{1,0:T(8,128)S(1)}, f32[128,512]{1,0:T(8,128)}, u32[]{:S(2)}) copy-start(f32[128,512]{1,0:T(8,128)} %z_ref.1) | copy-start | bytes 786436
  0.7 61.8 %copy-start.2 = (f32[128,512]{1,0:T(8,128)S(1)}, f32[128,512]{1,0:T(8,128)}, u32[]{:S(2)}) copy-start(f32[128,512]{1,0:T(8,128)} %s_ref.1) | copy-start | bytes 786436

commit v4 on v3

--- a/solution.py
+++ b/solution.py
@@ -23,8 +23,9 @@
 F32 = jnp.float32
 BF16 = jnp.bfloat16
 MESH = pl.DeviceIdType.MESH
-N_MSG = 160
+N_MSG = 192
 C_ROWS = 80
+CHUNKS = (48, 32)
 AB = 4 * C_ROWS
 R = (HV - AB) // 2
 Q = R // 2
@@ -35,10 +36,9 @@
     values_out, grad_out,
     z_ref, x_ref, tok, cot, cot_t, wts, gt,
     relay1, direct1, summed1, stage1, g1f, g1b, relay2, direct2, summed2, stage2,
-    c_f, c_b, c_recv,
-    zc_half, zc_recv, zc_stage,
     plane, zstage, zrecv, gfull, acc, vrecv,
     send_sem, recv_sem, tok_local, tok_send, tok_recv, in_sem,
+    *chunk_refs,
 ):
     zl = lax.axis_index("replica")
     index = lax.axis_index("fsdp")
@@ -66,7 +66,9 @@
 
     z_peers = [z_dev(z_plus(k)) for k in range(1, 8)]
     z_side = [z_dev(z_plus(1)), z_dev(z_plus(-1))]
-    mirror = z_dev(7 - z_now)
+    at_cut = lax.rem(zl, 3) == 0
+    outward = 2 * (zl // 2) - 1
+    outer, inner = z_dev(z_plus(outward)), z_dev(z_plus(-outward))
 
     def plane_plus(k):
         return lax.rem(yc * 4 + xc + k, 16)
@@ -170,8 +172,14 @@
             own = block(p, first[p], second[p], h, 64 * p, 64)
             for d in (0, 1):
                 ag[st, p, 0, d] = message(own, own, first_side[p][d])
+    def spread_own(st):
         for p in (0, 1):
             spread(st, p, 0)
+
+    def spread_next(st):
+        for p in (0, 1):
+            for item in (-1, 1):
+                spread(st, p, item)
 
     def ag1(st):
         h = half_of[st]
@@ -182,7 +190,6 @@
                 arrived(ag[st, p, 0, d], block(p, src_f, s, h, r0, 64))
                 part = block(p, src_f, s, h, r0 + 32 * d, 32)
                 ag[st, p, 1, d] = message(part, part, first_side[p][d])
-                spread(st, p, -1 + 2 * d)
 
     def ag2(st):
         h = half_of[st]
@@ -213,71 +220,80 @@
 
     zc = {}
 
-    def c_row(z):
-        return pl.multiple_of(lax.rem(z, 4) * C_ROWS, 16)
+    starts = [sum(CHUNKS[:c]) for c in range(len(CHUNKS))]
+    chunk = [chunk_refs[6 * c:6 * c + 6] for c in range(len(CHUNKS))]
+
+    def c_row(z, c):
+        return pl.ds(pl.multiple_of(lax.rem(z, 4) * C_ROWS + starts[c], 16), CHUNKS[c])
 
     def zc1(c):
         dest = z_plus(4)
         for d in (0, 1):
-            half = gt.at[pl.ds(2 * c, 2), dest // 4, pl.ds(2 * d, 2), pl.ds(c_row(dest), C_ROWS), :]
-            zc[1, d, c] = message(half, zc_half.at[d, c], z_side[d])
+            half = gt.at[:, dest // 4, pl.ds(2 * d, 2), c_row(dest, c), :]
+            zc[1, d, c] = message(half, chunk[c][0].at[d], z_side[d])
 
     def zc_step(s, c):
+        zc_half, zc_recv, zc_stage = chunk[c][:3]
         for d in (0, 1):
             dest = z_plus((5 - s) * (1 - 2 * d))
-            h, row = dest // 4, c_row(dest)
+            h, row = dest // 4, c_row(dest, c)
             if s == 2:
-                arrived(zc[1, d, c], zc_half.at[d, c])
-
-                @pl.loop(0, 4)
+                arrived(zc[1, d, c], zc_half.at[d])
+
+                @pl.loop(0, 8)
                 def _(i):
                     y, x = i // 2, lax.rem(i, 2)
-                    mine = gt[2 * c + y, h, 2 * d + x, pl.ds(row, C_ROWS), :].astype(F32)
-                    got = zc_half[d, c, y, x].astype(F32)
-                    zc_stage[0, d, c, y, 2 * d + x] = (mine + got).astype(BF16)
+                    mine = gt[y, h, 2 * d + x, row, :].astype(F32)
+                    got = zc_half[d, y, x].astype(F32)
+                    zc_stage[0, d, y, 2 * d + x] = (mine + got).astype(BF16)
                     other = 2 * (1 - d) + x
-                    zc_stage[0, d, c, y, other] = gt[2 * c + y, h, other, pl.ds(row, C_ROWS), :]
+                    zc_stage[0, d, y, other] = gt[y, h, other, row, :]
             else:
-                arrived(zc[s - 1, d, c], zc_recv.at[s - 3, d, c])
-
-                @pl.loop(0, 8)
+                arrived(zc[s - 1, d, c], zc_recv.at[s - 3, d])
+
+                @pl.loop(0, 16)
                 def _(i):
                     y, x = i // 4, lax.rem(i, 4)
-                    mine = gt[2 * c + y, h, x, pl.ds(row, C_ROWS), :].astype(F32)
-                    got = zc_recv[s - 3, d, c, y, x].astype(F32)
-                    zc_stage[s - 2, d, c, y, x] = (mine + got).astype(BF16)
-
-            zc[s, d, c] = message(zc_stage.at[s - 2, d, c], zc_recv.at[s - 2, d, c], z_side[d])
+                    mine = gt[y, h, x, row, :].astype(F32)
+                    got = zc_recv[s - 3, d, y, x].astype(F32)
+                    zc_stage[s - 2, d, y, x] = (mine + got).astype(BF16)
+
+            zc[s, d, c] = message(zc_stage.at[s - 2, d], zc_recv.at[s - 2, d], z_side[d])
 
     def zc_final(c):
+        _, zc_recv, _, c_f, c_b, _ = chunk[c]
         for d in (0, 1):
-            arrived(zc[4, d, c], zc_recv.at[2, d, c])
-        row = c_row(z_now)
-
-        @pl.loop(0, 8)
+            arrived(zc[4, d, c], zc_recv.at[2, d])
+        row = c_row(z_now, c)
+
+        @pl.loop(0, 16)
         def _(i):
             y, x = i // 4, lax.rem(i, 4)
             total = (
-                gt[2 * c + y, zh, x, pl.ds(row, C_ROWS), :].astype(F32)
-                + zc_recv[2, 0, c, y, x].astype(F32)
-                + zc_recv[2, 1, c, y, x].astype(F32)
+                gt[y, zh, x, row, :].astype(F32)
+                + zc_recv[2, 0, y, x].astype(F32)
+                + zc_recv[2, 1, y, x].astype(F32)
             )
-            c_f[2 * c + y, x] = total
-            c_b[2 * c + y, x] = total.astype(BF16)
-
-    def c_send():
-        out = []
+            c_f[y, x] = total
+            c_b[y, x] = total.astype(BF16)
+
+    c_msgs = {}
+    shares = {}
+
+    def c_send(c):
+        c_b, c_recv = chunk[c][4:]
         for k in range(1, 16):
             i = plane_plus(k)
-            out.append(message(c_b.at[i // 4, lax.rem(i, 4)], c_recv.at[k - 1], plane_peers[k - 1]))
-        return out
-
-    def c_end(msgs):
+            c_msgs[c, k] = message(c_b.at[i // 4, lax.rem(i, 4)], c_recv.at[k - 1], plane_peers[k - 1])
+
+    def c_end(c):
+        c_f, _, c_recv = chunk[c][3:]
         total = c_f[yc, xc]
-        for k in range(15):
-            arrived(msgs[k], c_recv.at[k])
-            total = total + c_recv[k].astype(F32)
-        gfull[pl.ds(c_row(z_now), C_ROWS), :] = total
+        for k in range(1, 16):
+            arrived(c_msgs[c, k], c_recv.at[k - 1])
+            total = total + c_recv[k - 1].astype(F32)
+        gfull[c_row(z_now, c), :] = total
+        share(c)
 
     def nxt(c, d):
         return mod4(c + 1 - 2 * d)
@@ -307,7 +323,7 @@
                 self.m[p, 2, d] = message(stage.at[p, d], summed.at[p, d], first_side[p][d])
 
         def turn(self, p):
-            _, dirc, summed, _, gf, gb, rel2, dir2 = self.bufs[:8]
+            _, dirc, summed, _, gf, gb, rel2 = self.bufs[:7]
             for d in (0, 1):
                 arrived(self.m[p, 1, d], dirc.at[p, d])
                 arrived(self.m[p, 2, d], summed.at[p, d])
@@ -321,11 +337,15 @@
                     )
                     gf[p, i, h] = total
                     gb[p, i, h] = total.astype(BF16)
-            s = second[p]
-            for d in (0, 1):
-                self.m[p, 3, d] = message(gb.at[p, mod4(s + 2), d], rel2.at[p, d], second_side[p][d])
-            for d in (0, 1):
-                self.m[p, 4, d] = message(gb.at[p, nxt(s, d), 1 - d], dir2.at[p, d], second_side[p][d])
+            for d in (0, 1):
+                src = gb.at[p, mod4(second[p] + 2), d]
+                self.m[p, 3, d] = message(src, rel2.at[p, d], second_side[p][d])
+
+        def turn2(self, p):
+            gb, _, dir2 = self.bufs[5:8]
+            for d in (0, 1):
+                src = gb.at[p, nxt(second[p], d), 1 - d]
+                self.m[p, 4, d] = message(src, dir2.at[p, d], second_side[p][d])
 
         def mid2(self, p):
             gf, _, rel2, _, summed2, stage2_ = self.bufs[4:]
@@ -375,6 +395,15 @@
         out = jnp.dot(lhs, wts[y, h].reshape(512, 512), preferred_element_type=F32)
         acc[m] = out if (st, y) == (0, 0) else acc[m] + out
 
+    def values2(st, y, m):
+        h = half_of[st]
+        cols = pl.ds(pl.multiple_of(h * 512, 512), 512)
+        total = acc[m]
+        for k in (0, 1):
+            rhs = wts[y + k, h].reshape(512, 512)
+            total = total + jnp.dot(tok[y + k, m, :, cols], rhs, preferred_element_type=F32)
+        acc[m] = total
+
     def z_send():
         out = []
         for k in range(1, 8):
@@ -388,16 +417,48 @@
         for k in range(7):
             arrived(msgs[k], zrecv.at[k])
             total = total + zrecv[k].astype(F32)
-        gfull[pl.ds(pl.multiple_of(AB + zl * Q, 16), Q), :] = total
-
-    def share(base, n):
-        rows = gfull.at[pl.ds(pl.multiple_of(base + zl * n, 16), n), :]
-        return [message(rows, rows, (lax.rem(zl + k, 4), index)) for k in range(1, 4)]
-
-    def shared(base, n, msgs):
+        gfull[rows_of(zl, "ab"), :] = total
+        share("ab")
+
+    def rows_of(z, part):
+        if part == "ab":
+            return pl.ds(pl.multiple_of(AB + lax.rem(z, 4) * Q, 16), Q)
+        return c_row(z, part)
+
+    def share(part):
+        rows = gfull.at[rows_of(zl, part), :]
         for k in range(1, 4):
-            row = pl.multiple_of(base + lax.rem(zl + 4 - k, 4) * n, 16)
-            arrived(msgs[k - 1], gfull.at[pl.ds(row, n), :])
+            shares[part, k] = message(rows, rows, (lax.rem(zl + k, 4), index))
+
+    def shared(part):
+        for k in range(1, 4):
+            arrived(shares[part, k], gfull.at[rows_of(zl + 4 - k, part), :])
+
+    def cut_copy(n, src, dev):
+        m = N_MSG - 2 + n
+        return pltpu.make_async_remote_copy(
+            src_ref=src, dst_ref=src, send_sem=send_sem.at[m], recv_sem=recv_sem.at[m],
+            device_id=dev, device_id_type=MESH,
+        )
+
+    own_block = wts.at[yc, zh, xc]
+    other_block = wts.at[yc, 1 - zh, xc]
+
+    def cut_send():
+        @pl.when(at_cut)
+        def _():
+            cut_copy(0, own_block, outer).start()
+
+    def cut_forward():
+        @pl.when(at_cut)
+        def _():
+            cut_copy(0, other_block, outer).wait_recv()
+            cut_copy(1, other_block, inner).start()
+
+    def cut_end():
+        @pl.when(jnp.logical_not(at_cut))
+        def _():
+            cut_copy(1, other_block, outer).wait_recv()
 
     def ab_start(which):
         for p in (0, 1):
@@ -413,94 +474,108 @@
                 plane[h, R * p:R * (p + 1), :] = total
                 zstage[h, R * p:R * (p + 1), :] = total.astype(BF16)
 
+    def finish_sends(lo, hi):
+        for copy in sends[lo:hi]:
+            copy.wait_send()
+
+    def finish_early():
+        finish_sends(0, early)
+
+        @pl.when(at_cut)
+        def _():
+            cut_copy(0, own_block, outer).wait_send()
+            cut_copy(1, other_block, inner).wait_send()
+
+        @pl.loop(0, 32)
+        def _(t):
+            remote_tok(t).wait_send()
+
     cot_msg = message(cot_hbm, cot.at[1], partner)
     ag0(0)
+    cut_send()
 
     @pl.loop(0, 32)
     def _(t):
         remote_tok(t).start()
 
-    own = wts.at[yc, zh, xc]
-    mirror_msg = message(own, own, mirror)
     cot_local.wait()
+    cot_t[:, :512] = cot[0].T
     arrived(cot_msg, cot.at[1])
-    for k in (0, 1):
-        cot_t[:, 512 * k:512 * (k + 1)] = cot[k].T
+    cot_t[:, 512:] = cot[1].T
     grad(0, 2)
+    spread_own(0)
     grad(2, 4)
-    zc1(0)
     grad(4, 6)
     grad(6, 8)
     zc1(1)
+    zc1(0)
     ag1(0)
+    spread_next(0)
+    cut_forward()
+    ag3(0, (0,))
     grad(8, 10)
     grad(10, 12)
     grad(12, 14)
     grad(14, 16)
     ab_start(0)
-    zc_step(2, 0)
+    ab_start(1)
     ag2(0)
-    ag3(0, (0,))
-    ab_start(1)
-    arrived(mirror_msg, wts.at[yc, 1 - zh, xc])
-    ag0(1)
     zc_step(2, 1)
     ag3(0, (-1, 1))
+    zc_step(2, 0)
+    cut_end()
+    ag0(1)
+    spread_own(1)
+    ag3(0, (2,))
+    zc_step(3, 1)
+    ab_all(ab.mid)
     zc_step(3, 0)
-    zc_step(3, 1)
-    ag3(0, (2,))
-    ab_all(ab.mid)
-    ag1(1)
-    ag3(1, (0,))
     ag4(0)
     values(0, 0, 0)
+    ag1(1)
+    spread_next(1)
     values(0, 0, 1)
     values(0, 1, 0)
     values(0, 1, 1)
     values(0, 2, 0)
     values(0, 2, 1)
-    zc_step(4, 0)
     values(0, 3, 0)
     values(0, 3, 1)
     zc_step(4, 1)
+    ab_all(ab.turn)
     ag2(1)
-    ab_all(ab.turn)
+    ag3(1, (0,))
+    ab_all(ab.turn2)
+    zc_step(4, 0)
     ag3(1, (-1, 1))
-    ag3(1, (2,))
     ab_all(ab.mid2)
-    zc_final(0)
     zc_final(1)
+    c_send(1)
     ab_end()
     z_msgs = z_send()
-    c_msgs = c_send()
+    ag3(1, (2,))
+    zc_final(0)
+    c_send(0)
+    c_end(1)
     ag4(1)
-    values(1, 0, 1)
-    values(1, 1, 1)
-    values(1, 2, 1)
-    values(1, 3, 1)
-    values(1, 0, 0)
-    values(1, 1, 0)
-    values(1, 2, 0)
-    values(1, 3, 0)
+    values2(1, 0, 1)
+    values2(1, 2, 1)
     z_end(z_msgs)
-    ab_share = share(AB, Q)
     vmsg = message(acc.at[1], vrecv, partner)
-    c_end(c_msgs)
-    c_share = share(0, C_ROWS)
+    values2(1, 0, 0)
+    values2(1, 2, 0)
+    c_end(0)
+    early = counter[0] - 30
+    finish_early()
     arrived(vmsg, vrecv)
     values_out[...] = ((acc[0] + vrecv[...]) * NORM).astype(BF16)
-    shared(0, C_ROWS, c_share)
-    shared(AB, Q, ab_share)
+    for part in (*range(2), "ab"):
+        shared(part)
     grad_out[...] = gfull[...]
 
-    for copy in sends:
-        copy.wait_send()
-
-    @pl.loop(0, 32)
-    def _(t):
-        remote_tok(t).wait_send()
-
-    assert counter[0] <= N_MSG
+    finish_sends(early, len(sends))
+
+    assert counter[0] <= N_MSG - 2
 
 
 def finish(values_ref, grad_ref, z_ref, x_ref, s_ref, values_out, z_out, x_out, s_out):
@@ -530,6 +605,16 @@
             + [pltpu.VMEM((2, 4, 2, r, 128), F32), pltpu.VMEM((2, 4, 2, r, 128), BF16)]
             + [pltpu.VMEM((2, 2, r, 128), BF16)] * 4
         )
+
+    def chunk_bufs(r):
+        return [
+            pltpu.VMEM((2, 4, 2, r, 128), BF16),
+            pltpu.VMEM((3, 2, 4, 4, r, 128), BF16),
+            pltpu.VMEM((3, 2, 4, 4, r, 128), BF16),
+            pltpu.VMEM((4, 4, r, 128), F32),
+            pltpu.VMEM((4, 4, r, 128), BF16),
+            pltpu.VMEM((15, r, 128), BF16),
+        ]
 
     values, gradient = pl.pallas_call(
         kernel,
@@ -545,12 +630,6 @@
             pltpu.VMEM((4, 2, 4, 128, 512), BF16),
             pltpu.VMEM((4, 2, 4, 512, 128), BF16),
         ] + plane_bufs(R) + [
-            pltpu.VMEM((4, 4, C_ROWS, 128), F32),
-            pltpu.VMEM((4, 4, C_ROWS, 128), BF16),
-            pltpu.VMEM((15, C_ROWS, 128), BF16),
-            pltpu.VMEM((2, 2, 2, 2, C_ROWS, 128), BF16),
-            pltpu.VMEM((3, 2, 2, 2, 4, C_ROWS, 128), BF16),
-            pltpu.VMEM((3, 2, 2, 2, 4, C_ROWS, 128), BF16),
             pltpu.VMEM((2, 2 * R, 128), F32),
             pltpu.VMEM((2, 2 * R, 128), BF16),
             pltpu.VMEM((7, Q, 128), BF16),
@@ -563,7 +642,7 @@
             dma((32,)),
             dma((32,)),
             dma((3,)),
-        ],
+        ] + [ref for r in CHUNKS for ref in chunk_bufs(r)],
         compiler_params=pltpu.CompilerParams(
             collective_id=0, has_side_effects=True, vmem_limit_bytes=48 * 1024 * 1024
         ),

time: 63.9 us -> 62.3 us (0.975)
  Pallas kernels: 63.1 us -> 61.5 us
    pallas_call x1, Pallas kernels: 61.8 us -> 60.1 us  [local(): pl.pallas_call(kernel, out_shape=(vals, jax.ShapeDtypeStruct((HV, 128), F...]
where the time goes in v4:
time: 62.3 us; the launch traced here: 62.2 us
  Pallas kernels  61.5 us (99%)
  between operations  0.69 us (1%)
    pallas_call x1, Pallas kernels, local(): pl.pallas_call(kernel, out_shape=(vals, jax.ShapeDtypeStruct((HV, 128), F...  60.1 us
    pallas_call x1, Pallas kernels, local(): pl.pallas_call(finish, out_shape=(vals, shard, shard, shard), in_specs=[v...  1.34 us

profile of v4, /device:TPU:32, one launch (start us, length us, event | category | flops | bytes accessed | tf_op | source)
XLA Modules:
  0.0 62.2 jit_solution(13731551975346001168)
XLA Ops:
  0.6 0.0 copy-start.1
  0.6 0.0 copy-start
  0.7 0.0 copy-start.2
  0.7 60.1 %shard_map.84 = (bf16[512,512]{1,0:T(8,128)(2,1)S(1)}, f32[512,128]{1,0:T(8,128)S(1)}) custom-call(bf16[512,8192]{1,0:T(8,128)(2,1)} %tokens.1, bf16[512,512]{1,0:T(8,128)(2,1)} %cot_hbm.1, f32[128,512]{1,0:T(8,128)} %z_ref.1, f32[128,512]{1,0:T(8,128)} %x_ref.1), custom_call_target="tpu_custom_call" | custom-call | tf_op jit(solution)/shard_map/pallas_call | solution.py:619
  60.8 0.0 copy-done.1
  60.8 0.0 copy-done
  60.8 0.0 copy-done.2
  60.8 1.3 %shard_map.85 = (bf16[512,512]{1,0:T(8,128)(2,1)}, f32[128,512]{1,0:T(8,128)}, f32[128,512]{1,0:T(8,128)}, f32[128,512]{1,0:T(8,128)}) custom-call(bf16[512,512]{1,0:T(8,128)(2,1)S(1)} %get-tuple-element.6.values_ref, f32[512,128]{1,0:T(8,128)S(1)} %get-tuple-element.7.grad_ref, f32[128,512]{1,0:T(8,128)S(1)} %copy-done, f32[128,512]{1,0:T(8,128)S(1)} %copy-done.1, ...), custom_call_target="tpu_custom_call" | custom-call | tf_op jit(solution)/shard_map/pallas_call | solution.py:650
Async XLA Ops:
  0.6 60.2 %copy-start.1 = (f32[128,512]{1,0:T(8,128)S(1)}, f32[128,512]{1,0:T(8,128)}, u32[]{:S(2)}) copy-start(f32[128,512]{1,0:T(8,128)} %x_ref.1) | copy-start | bytes 786436
  0.6 60.2 %copy-start = (f32[128,512]{1,0:T(8,128)S(1)}, f32[128,512]{1,0:T(8,128)}, u32[]{:S(2)}) copy-start(f32[128,512]{1,0:T(8,128)} %z_ref.1) | copy-start | bytes 786436
  0.7 60.2 %copy-start.2 = (f32[128,512]{1,0:T(8,128)S(1)}, f32[128,512]{1,0:T(8,128)}, u32[]{:S(2)}) copy-start(f32[128,512]{1,0:T(8,128)} %s_ref.1) | copy-start | bytes 786436

commit v5 on v4

--- a/solution.py
+++ b/solution.py
@@ -502,69 +502,69 @@
     cot_t[:, :512] = cot[0].T
     arrived(cot_msg, cot.at[1])
     cot_t[:, 512:] = cot[1].T
+    spread_own(0)
     grad(0, 2)
-    spread_own(0)
     grad(2, 4)
     grad(4, 6)
     grad(6, 8)
     zc1(1)
-    zc1(0)
     ag1(0)
     spread_next(0)
-    cut_forward()
-    ag3(0, (0,))
+    zc1(0)
     grad(8, 10)
     grad(10, 12)
     grad(12, 14)
     grad(14, 16)
     ab_start(0)
-    ab_start(1)
+    cut_forward()
     ag2(0)
     zc_step(2, 1)
+    ag3(0, (0,))
+    ab_start(1)
+    zc_step(2, 0)
     ag3(0, (-1, 1))
-    zc_step(2, 0)
+    ag3(0, (2,))
     cut_end()
     ag0(1)
     spread_own(1)
-    ag3(0, (2,))
+    ab_all(ab.mid)
     zc_step(3, 1)
-    ab_all(ab.mid)
-    zc_step(3, 0)
     ag4(0)
     values(0, 0, 0)
-    ag1(1)
-    spread_next(1)
     values(0, 0, 1)
     values(0, 1, 0)
+    zc_step(3, 0)
     values(0, 1, 1)
     values(0, 2, 0)
     values(0, 2, 1)
     values(0, 3, 0)
     values(0, 3, 1)
+    ag3(1, (0,))
+    ag1(1)
+    spread_next(1)
+    ab_all(ab.turn)
+    ab_all(ab.turn2)
     zc_step(4, 1)
-    ab_all(ab.turn)
     ag2(1)
-    ag3(1, (0,))
-    ab_all(ab.turn2)
     zc_step(4, 0)
-    ag3(1, (-1, 1))
     ab_all(ab.mid2)
     zc_final(1)
     c_send(1)
+    ag3(1, (-1, 1))
+    ag3(1, (2,))
     ab_end()
     z_msgs = z_send()
-    ag3(1, (2,))
     zc_final(0)
     c_send(0)
     c_end(1)
     ag4(1)
     values2(1, 0, 1)
+    z_end(z_msgs)
     values2(1, 2, 1)
-    z_end(z_msgs)
     vmsg = message(acc.at[1], vrecv, partner)
     values2(1, 0, 0)
+    c_end(0)
     values2(1, 2, 0)
-    c_end(0)
     early = counter[0] - 30
     finish_early()
     arrived(vmsg, vrecv)

time: 62.3 us -> 61.7 us (level); the launches traced: 62.2 us -> 60.8 us
  Pallas kernels: 61.5 us -> 60.1 us
    pallas_call x1, Pallas kernels: 60.1 us -> 58.7 us  [local(): pl.pallas_call(kernel, out_shape=(vals, jax.ShapeDtypeStruct((HV, 128), F...]
where the time goes in v5:
time: 61.7 us; the launch traced here: 60.8 us
  Pallas kernels  60.1 us (97%)
  between operations  0.69 us (1%)
    pallas_call x1, Pallas kernels, local(): pl.pallas_call(kernel, out_shape=(vals, jax.ShapeDtypeStruct((HV, 128), F...  58.7 us
    pallas_call x1, Pallas kernels, local(): pl.pallas_call(finish, out_shape=(vals, shard, shard, shard), in_specs=[v...  1.34 us

profile of v5, /device:TPU:32, one launch (start us, length us, event | category | flops | bytes accessed | tf_op | source)
XLA Modules:
  0.0 60.8 jit_solution(6955469449063027949)
XLA Ops:
  0.6 0.0 copy-start.1
  0.6 0.0 copy-start
  0.7 0.0 copy-start.2
  0.7 58.7 %shard_map.84 = (bf16[512,512]{1,0:T(8,128)(2,1)S(1)}, f32[512,128]{1,0:T(8,128)S(1)}) custom-call(bf16[512,8192]{1,0:T(8,128)(2,1)} %tokens.1, bf16[512,512]{1,0:T(8,128)(2,1)} %cot_hbm.1, f32[128,512]{1,0:T(8,128)} %z_ref.1, f32[128,512]{1,0:T(8,128)} %x_ref.1), custom_call_target="tpu_custom_call" | custom-call | tf_op jit(solution)/shard_map/pallas_call | solution.py:619
  59.4 0.0 copy-done.1
  59.4 0.0 copy-done
  59.4 0.0 copy-done.2
  59.4 1.3 %shard_map.85 = (bf16[512,512]{1,0:T(8,128)(2,1)}, f32[128,512]{1,0:T(8,128)}, f32[128,512]{1,0:T(8,128)}, f32[128,512]{1,0:T(8,128)}) custom-call(bf16[512,512]{1,0:T(8,128)(2,1)S(1)} %get-tuple-element.6.values_ref, f32[512,128]{1,0:T(8,128)S(1)} %get-tuple-element.7.grad_ref, f32[128,512]{1,0:T(8,128)S(1)} %copy-done, f32[128,512]{1,0:T(8,128)S(1)} %copy-done.1, ...), custom_call_target="tpu_custom_call" | custom-call | tf_op jit(solution)/shard_map/pallas_call | solution.py:650
Async XLA Ops:
  0.6 58.8 %copy-start.1 = (f32[128,512]{1,0:T(8,128)S(1)}, f32[128,512]{1,0:T(8,128)}, u32[]{:S(2)}) copy-start(f32[128,512]{1,0:T(8,128)} %x_ref.1) | copy-start | bytes 786436
  0.6 58.8 %copy-start = (f32[128,512]{1,0:T(8,128)S(1)}, f32[128,512]{1,0:T(8,128)}, u32[]{:S(2)}) copy-start(f32[128,512]{1,0:T(8,128)} %z_ref.1) | copy-start | bytes 786436
  0.7 58.8 %copy-start.2 = (f32[128,512]{1,0:T(8,128)S(1)}, f32[128,512]{1,0:T(8,128)}, u32[]{:S(2)}) copy-start(f32[128,512]{1,0:T(8,128)} %s_ref.1) | copy-start | bytes 786436
